TPU v7x, 32 devices: a whole 2x2x4 slice. The times are simulated.
32 devices in a mesh: grp: 2 (over y), scen: 4 (over z), blk: 2 (over x), sub: 2 (over core).
Axes of the slice: x: 2, y: 2, z: 4, core: 2. Of those that a mesh axis runs over, the one named last changes fastest.
Arguments:
- block_matrices: float32 [8, 256, 128, 128], P(('grp', 'scen'), ('blk', 'sub')), parts along dimension 0, may hold values from -0.25 to 0.25
- slot_row_block: int32 [8, 256], P(('grp', 'scen'), ('blk', 'sub')), parts along dimension 0, may hold values from 0 to 7
- tile_column: int32 [8, 256], P(('grp', 'scen'), ('blk', 'sub')), parts along dimension 0, may hold values from 0 to 4127, as said below
- block_count: int32 [8, 4], P(('grp', 'scen'), ('blk', 'sub')), parts along dimension 0, may hold values from 8 to 64, as said below
- carbon_scenario: int32 [8], P(('grp', 'scen')), parts along dimension 0, may hold values from 0 to 23
- intensity: float32 [24, 32, 128], P(None, ('blk', 'sub')), may hold values from 0.2 to 2
- cost_first: float32 [8192, 128], P(('grp', 'scen', 'blk', 'sub')), parts along dimension 0, may hold values from -6 to 6
- lower_first: float32 [8192, 128], P(('grp', 'scen', 'blk', 'sub')), parts along dimension 0, may hold values from -1 to -0.2
- upper_first: float32 [8192, 128], P(('grp', 'scen', 'blk', 'sub')), parts along dimension 0, may hold values from 0.2 to 1
- cost_second: float32 [8, 32, 128], P(('grp', 'scen'), ('blk', 'sub')), parts along dimension 0, may hold values from -6 to 6
- upper_second: float32 [8, 32, 128], P(('grp', 'scen'), ('blk', 'sub')), parts along dimension 0, may hold values from 0.2 to 2
- row_bound: float32 [8, 32, 128], P(('grp', 'scen'), ('blk', 'sub')), parts along dimension 0, may hold values from -20 to 20
- first_start: float32 [8192, 128], P(('grp', 'scen', 'blk', 'sub')), parts along dimension 0, may hold values from -0.2 to 0.2
- second_start: float32 [8, 32, 128], P(('grp', 'scen'), ('blk', 'sub')), parts along dimension 0, may hold values from 0 to 0.2
- dual_start: float32 [8, 32, 128], P(('grp', 'scen'), ('blk', 'sub')), parts along dimension 0, may hold values from 0 to 1
Outputs:
- first_final: float32 [8192, 128], P(('grp', 'scen', 'blk', 'sub')), parts along dimension 0
- second_final: float32 [8, 32, 128], P(('grp', 'scen'), ('blk', 'sub')), parts along dimension 0
- dual_final: float32 [8, 32, 128], P(('grp', 'scen'), ('blk', 'sub')), parts along dimension 0
- residual_norm: float32 [6], P('grp'), parts along dimension 0
There are 2 independent parts, one for each index of `grp`. A program takes and returns all parts, laid end to end along the dimension named above; an argument that names none is the same for every part. Nothing has to cross between parts.
Inputs may be any that keep to these rules, and one draw needn't show every extreme that they name: `block_count`: each scenario has one index of blk and sub with all 64 slots used; the others use between 8 and 32. `tile_column`: values below 4096 name first-section column blocks, values from 4096 on second-section ones. Split the first-section blocks into 16 equal shards in order, and take the slots of one index of scen and of blk and sub together (64 of them, scenario by scenario). In every draw, on every such device, at most 4 of them name first-section blocks of one shard, and some shard is named by exactly 4.
All inputs are finite; a program needn't handle non-finite values.
Results may differ from a plain program's by a relative error of at most 0.0003.
Values sent between devices are 32-bit elements; how exact they have to be, the bound alone decides.
No kernel may reach another device: no remote copies, remote signals or barrier semaphores. Data moves between devices by JAX's collectives and lax.ppermute only.
A program may use at most 64 MiB of HBM per device.

v0:
```python
import jax
import jax.numpy as jnp
from jax import lax
from jax.sharding import PartitionSpec as P

ITERS = 3


precise = lax.Precision.HIGHEST
step_primal = 0.4
step_dual = 0.4


def forward_window(
    block_matrices,
    onehot,
    mask,
    tile_column,
    fetch_first,
    count_first,
    second_bar,
    offset,
    window_size,
):
    count_second = second_bar.shape[1]
    is_first = tile_column < count_first
    from_first = fetch_first(tile_column, offset, window_size)
    second_index = jnp.clip(tile_column - count_first, 0, count_second - 1)
    from_second = jax.vmap(lambda table, index: table[index])(second_bar, second_index)
    blocks = jnp.where(is_first[:, :, None], from_first, from_second)
    product = jnp.einsum("skij,skj->ski", block_matrices, blocks, precision=precise)
    product = product * mask[:, :, None]
    return jnp.einsum("skr,ski->sri", onehot, product, precision=precise)


def adjoint_window(
    block_matrices,
    onehot,
    mask,
    tile_column,
    dual,
    collect_first,
    count_first,
    count_second,
    offset,
    window_size,
):
    gathered = jnp.einsum("skr,sri->ski", onehot, dual, precision=precise)
    product = jnp.einsum("skij,ski->skj", block_matrices, gathered, precision=precise)
    product = product * mask[:, :, None]
    is_first = tile_column < count_first
    first_terms = collect_first(product, tile_column, offset, window_size)
    second_index = jnp.where(is_first, count_second, tile_column - count_first)
    scenario_index = lax.broadcasted_iota(jnp.int32, second_index.shape, 0)
    second_terms = (
        jnp.zeros((product.shape[0], count_second, product.shape[2]), jnp.float32)
        .at[scenario_index, second_index]
        .add(product, mode="drop")
    )
    return (first_terms, second_terms)


def shards(
    block_matrices,
    slot_row_block,
    tile_column,
    block_count,
    carbon_scenario,
    intensity,
    cost_first,
    lower_first,
    upper_first,
    cost_second,
    upper_second,
    row_bound,
    first_start,
    second_start,
    dual_start,
):
    scen_local, slots = slot_row_block.shape
    rows_local = row_bound.shape[1]
    tile_size = row_bound.shape[2]
    shard_first = cost_first.shape[0]
    owner_count = lax.axis_size(("scen", "blk", "sub"))
    count_first = shard_first * owner_count
    count_second = cost_second.shape[1] * lax.axis_size(("blk", "sub"))
    total_cells = scen_local * rows_local * tile_size * owner_count
    mask = (jnp.arange(slots, dtype=jnp.int32)[None, :] < block_count).astype(jnp.float32)
    onehot = (
        slot_row_block[:, :, None] == jnp.arange(rows_local, dtype=jnp.int32)[None, None, :]
    ).astype(jnp.float32)
    choose = (
        carbon_scenario[:, None] == jnp.arange(intensity.shape[0], dtype=jnp.int32)[None, :]
    ).astype(jnp.float32)
    cost_total = cost_second + jnp.einsum("sc,cbt->sbt", choose, intensity, precision=precise)
    first_shape = (count_first, tile_size)

    def collect_first(product, column_window, offset, width):
        first_index = jnp.where(column_window < count_first, column_window, count_first).reshape(-1)
        return (
            jnp.zeros(first_shape, jnp.float32)
            .at[first_index]
            .add(product.reshape(-1, tile_size), mode="drop")
        )

    def make_fetch(first_source):

        def fetch_first(column_window, offset, width):
            return first_source[jnp.clip(column_window, 0, count_first - 1)]

        return fetch_first

    cost_all, lower_all, upper_all, first_now = (
        lax.all_gather(cost_first, ("scen", "blk", "sub"), axis=0, tiled=True),
        lax.all_gather(lower_first, ("scen", "blk", "sub"), axis=0, tiled=True),
        lax.all_gather(upper_first, ("scen", "blk", "sub"), axis=0, tiled=True),
        lax.all_gather(first_start, ("scen", "blk", "sub"), axis=0, tiled=True),
    )
    second_now = second_start
    dual = dual_start
    squares = []
    for step_index in range(ITERS):
        grad_first_part, grad_second_part = adjoint_window(
            block_matrices,
            onehot,
            mask,
            tile_column,
            dual,
            collect_first,
            count_first,
            count_second,
            0,
            slots,
        )
        grad_second = lax.psum_scatter(
            grad_second_part, ("blk", "sub"), scatter_dimension=1, tiled=True
        )
        grad_first = lax.psum(grad_first_part, ("scen", "blk", "sub"))
        first_next = jnp.clip(
            first_now - step_primal * (cost_all - grad_first), lower_all, upper_all
        )
        first_source = 2.0 * first_next - first_now
        second_next = jnp.clip(
            second_now - step_primal * (cost_total - grad_second), 0.0, upper_second
        )
        second_bar = lax.all_gather(
            2.0 * second_next - second_now, ("blk", "sub"), axis=1, tiled=True
        )
        residual = row_bound - forward_window(
            block_matrices,
            onehot,
            mask,
            tile_column,
            make_fetch(first_source),
            count_first,
            second_bar,
            0,
            slots,
        )
        local_square = jnp.sum(residual * residual)
        squares.append(lax.psum(local_square, ("scen", "blk", "sub")))
        dual = jnp.maximum(dual + step_dual * residual, 0.0)
        first_now = first_next
        second_now = second_next
    totals = jnp.stack(squares)
    residual_norm = jnp.sqrt(totals / total_cells)
    offset = lax.axis_index(("scen", "blk", "sub")) * shard_first
    first_final = lax.dynamic_slice_in_dim(first_now, offset, shard_first, 0)
    return (first_final, second_now, dual, residual_norm)


def solution(mesh):
    return jax.shard_map(
        shards,
        mesh=mesh,
        in_specs=(
            P(("grp", "scen"), ("blk", "sub"), None, None),
            P(("grp", "scen"), ("blk", "sub")),
            P(("grp", "scen"), ("blk", "sub")),
            P(("grp", "scen"), ("blk", "sub")),
            P(("grp", "scen")),
            P(None, ("blk", "sub"), None),
            P(("grp", "scen", "blk", "sub"), None),
            P(("grp", "scen", "blk", "sub"), None),
            P(("grp", "scen", "blk", "sub"), None),
            P(("grp", "scen"), ("blk", "sub"), None),
            P(("grp", "scen"), ("blk", "sub"), None),
            P(("grp", "scen"), ("blk", "sub"), None),
            P(("grp", "scen", "blk", "sub"), None),
            P(("grp", "scen"), ("blk", "sub"), None),
            P(("grp", "scen"), ("blk", "sub"), None),
        ),
        out_specs=(
            P(("grp", "scen", "blk", "sub"), None),
            P(("grp", "scen"), ("blk", "sub"), None),
            P(("grp", "scen"), ("blk", "sub"), None),
            P("grp"),
        ),
        check_vma=False,
    )
```

profile of v0, /device:TPU:0, one launch (start us, length us, event | category | flops | bytes accessed | tf_op | source)
XLA Modules:
  0.0 587.8 jit_solution(10443737884723280404)
XLA Ops:
  8.5 0.9 fusion.66
  9.5 5.3 fusion.10
  14.8 2.3 scatter_custom_fusion
  22.7 13.2 %all-reduce.1 = f32[1,32,128]{2,1,0:T(8,128)S(1)} all-reduce(f32[1,32,128]{2,1,0:T(8,128)S(1)} %bitcast.135), channel_id=2, replica_groups=mesh['grp'=2,'scen'=4,'blk'=2,'sub'=2] {'blk','sub'}, use_global_device_ids=true, to_apply=%region_3.4.clone | all-reduce | flops 4096 | bytes 32768
  36.1 5.2 all_gather.25
  42.1 75.8 %all-reduce.9.cloned.1.call-done = f32[4096,128]{1,0:T(8,128)} async-done(((f32[4096,128]{1,0:T(8,128)}), f32[4096,128]{1,0:T(8,128)}) %all-reduce.9.cloned.1.call-update) | async-done | bytes 2097168 | tf_op jit(solution)/shard_map/psum | solution.py:138
  117.9 43.1 %all-gather.11.cloned.1.call-done = f32[4096,128]{1,0:T(8,128)} async-done(((f32[256,128]{1,0:T(8,128)}), f32[4096,128]{1,0:T(8,128)}) %all-gather.11.cloned.1.call-update) | async-done | bytes 2097168 | tf_op jit(solution)/shard_map/all_gather | solution.py:114
  160.9 42.6 %all-gather.5.cloned.1.call-done = f32[4096,128]{1,0:T(8,128)} async-done(((f32[256,128]{1,0:T(8,128)}), f32[4096,128]{1,0:T(8,128)}) %all-gather.5.cloned.1.call-update) | async-done | bytes 2097168 | tf_op jit(solution)/shard_map/all_gather | solution.py:116
  203.6 42.5 %all-gather.7.cloned.1.call-done = f32[4096,128]{1,0:T(8,128)} async-done(((f32[256,128]{1,0:T(8,128)}), f32[4096,128]{1,0:T(8,128)}) %all-gather.7.cloned.1.call-update) | async-done | bytes 2097168 | tf_op jit(solution)/shard_map/all_gather | solution.py:115
  246.0 42.4 %all-gather.9.cloned.1.call-done = f32[4096,128]{1,0:T(8,128)} async-done(((f32[256,128]{1,0:T(8,128)}), f32[4096,128]{1,0:T(8,128)}) %all-gather.9.cloned.1.call-update) | async-done | bytes 2097168 | tf_op jit(solution)/shard_map/all_gather | solution.py:117
  288.5 5.9 %multiply_subtract_fusion.2 = (f32[4096,128]{1,0:T(8,128)S(1)}, f32[4096,128]{1,0:T(8,128)}) fusion(f32[4096,128]{1,0:T(8,128)} %all-gather.9.cloned.1.call-done, f32[4096,128]{1,0:T(8,128)} %all-gather.5.cloned.1.call-done, f32[4096,128]{1,0:T(8,128)} %all-gather.7.cloned.1.call-done, f32[4096,128]{1,0:T(8,128)} %all-gather.11.cloned.1.call-done, ...), kind=kLoop, calls=%fused_computation.28 | loop fusion | flops 3670016 | bytes 14680064 | tf_op jit(solution)/shard_map/sub | solution.py:142
  295.1 8.5 %fusion.8 = f32[64,1,128]{2,1,0:T(1,128)S(1)} fusion(f32[64,128,1]{1,2,0:T(1,128)S(1)} %bitcast.130, f32[1,64,128,128]{3,2,1,0:T(8,128)} %param.15), kind=kOutput, calls=%fused_computation.20 | convolution fusion | flops 12582912 | bytes 4259840 | tf_op jit(solution)/shard_map/skij,skj->ski/dot_general | solution.py:31
  304.1 3.7 fusion.6
  307.7 2.3 scatter_custom_fusion.2
  311.0 10.4 %all-reduce.2 = f32[1,32,128]{2,1,0:T(8,128)S(1)} all-reduce(f32[1,32,128]{2,1,0:T(8,128)S(1)} %bitcast.137), channel_id=3, replica_groups=mesh['grp'=2,'scen'=4,'blk'=2,'sub'=2] {'blk','sub'}, use_global_device_ids=true, to_apply=%region_7.8.clone | all-reduce | flops 4096 | bytes 32768
  321.4 5.4 all_gather.26
  327.5 79.2 %all-reduce.11.cloned.1.call-done = f32[4096,128]{1,0:T(8,128)} async-done(((f32[4096,128]{1,0:T(8,128)}), f32[4096,128]{1,0:T(8,128)}) %all-reduce.11.cloned.1.call-update) | async-done | bytes 2097168 | tf_op jit(solution)/shard_map/psum | solution.py:138
  406.8 6.2 %multiply_subtract_fusion.1 = (f32[4096,128]{1,0:T(8,128)}, f32[4096,128]{1,0:T(8,128)}) fusion(f32[4096,128]{1,0:T(8,128)} %get-tuple-element.19, f32[4096,128]{1,0:T(8,128)} %all-gather.5.cloned.1.call-done, f32[4096,128]{1,0:T(8,128)} %all-gather.7.cloned.1.call-done, f32[4096,128]{1,0:T(8,128)S(1)} %copy-done.3, f32[4096,128]{1,0:T(8,128)} %all-reduce.11.cloned.1.call-done), kind=kLoop, calls=%fused_computation.26 | loop fusion | flops 3670016 | bytes 14680064 | tf_op jit(solution)/shard_map/sub | solution.py:142
  413.0 2.2 gather_fusion.1
  415.2 8.5 %fusion.4 = f32[64,1,128]{2,1,0:T(1,128)S(1)} fusion(f32[64,128,1]{1,2,0:T(1,128)S(1)} %bitcast.131, f32[1,64,128,128]{3,2,1,0:T(8,128)} %param.15), kind=kOutput, calls=%fused_computation.16 | convolution fusion | flops 12582912 | bytes 4259840 | tf_op jit(solution)/shard_map/skij,skj->ski/dot_general | solution.py:31
  424.2 3.7 fusion.2
  427.9 2.3 scatter_custom_fusion.4
  431.1 10.6 %all-reduce.3 = f32[1,32,128]{2,1,0:T(8,128)S(1)} all-reduce(f32[1,32,128]{2,1,0:T(8,128)S(1)} %bitcast.136), channel_id=4, replica_groups=mesh['grp'=2,'scen'=4,'blk'=2,'sub'=2] {'blk','sub'}, use_global_device_ids=true, to_apply=%region_11.12.clone | all-reduce | flops 4096 | bytes 32768
  442.2 5.4 all_gather.27
  448.4 79.0 %all-reduce.13.cloned.1.call-done = f32[4096,128]{1,0:T(8,128)} async-done(((f32[4096,128]{1,0:T(8,128)}), f32[4096,128]{1,0:T(8,128)}) %all-reduce.13.cloned.1.call-update) | async-done | bytes 2097168 | tf_op jit(solution)/shard_map/psum | solution.py:138
  527.5 6.2 %multiply_subtract_fusion = (f32[4096,128]{1,0:T(8,128)}, f32[4096,128]{1,0:T(8,128)}) fusion(f32[4096,128]{1,0:T(8,128)} %get-tuple-element.14, f32[4096,128]{1,0:T(8,128)} %all-gather.5.cloned.1.call-done, f32[4096,128]{1,0:T(8,128)} %all-gather.7.cloned.1.call-done, f32[4096,128]{1,0:T(8,128)S(1)} %copy-done.3, f32[4096,128]{1,0:T(8,128)} %all-reduce.13.cloned.1.call-done), kind=kLoop, calls=%fused_computation.24 | loop fusion | flops 3670016 | bytes 14680064 | tf_op jit(solution)/shard_map/sub | solution.py:142
  533.7 2.2 gather_fusion.2
  535.9 8.3 %fusion = f32[64,1,128]{2,1,0:T(1,128)S(1)} fusion(f32[64,128,1]{1,2,0:T(1,128)S(1)} %bitcast.129, f32[1,64,128,128]{3,2,1,0:T(8,128)} %param.15), kind=kOutput, calls=%fused_computation.12 | convolution fusion | flops 12582912 | bytes 4259840 | tf_op jit(solution)/shard_map/skij,skj->ski/dot_general | solution.py:31
  544.2 1.6 multiply_reduce_fusion.2
  545.8 1.6 constant_dynamic-slice_fusion
  547.4 31.1 %all-reduce.4 = (f32[1]{0:T(128)}, f32[1]{0:T(128)}, f32[1]{0:T(128)}) all-reduce(f32[1]{0:T(128)} %bitcast.54, f32[1]{0:T(128)} %bitcast.53, f32[1]{0:T(128)} %bitcast.52), channel_id=1, replica_groups=mesh['grp'=2,'scen'=4,'blk'=2,'sub'=2] {'scen','blk','sub'}, use_global_device_ids=true, to_apply=%region_17.18 | all-reduce | flops 3 | bytes 24 | tf_op jit(solution)/shard_map/psum | solution.py:161
  578.4 2.5 fusion.82
  (66 shorter events, 11.7 us)
Async XLA Ops:
  7.2 28.7 %copy-start = (f32[24,8,128]{2,1,0:T(8,128)S(1)}, f32[24,8,128]{2,1,0:T(8,128)}, u32[]{:S(2)}) copy-start(f32[24,8,128]{2,1,0:T(8,128)} %param.20) | copy-start | bytes 294916
  7.2 110.7 %all-reduce.9.cloned.1.call-start = ((), (), s32[]{:S(2)}) async-start(), calls=%async_computation.4 | async-start | bytes 4194304 | tf_op jit(solution)/shard_map/psum | solution.py:138
  14.8 5.1 copy-start.9
  14.8 6.7 %copy-start.11 = (u32[32]{0:T(128)S(1)}, u32[32]{0:T(128)}, u32[]{:S(2)}) copy-start(u32[32]{0:T(128)} %constant.109) | copy-start | bytes 388
  14.8 21.3 %copy-start.4 = (f32[1,8,128]{2,1,0:T(8,128)S(1)}, f32[1,8,128]{2,1,0:T(8,128)}, u32[]{:S(2)}) copy-start(f32[1,8,128]{2,1,0:T(8,128)} %param.25) | copy-start | bytes 12292
  14.8 21.3 %copy-start.7 = (f32[1,8,128]{2,1,0:T(8,128)S(1)}, f32[1,8,128]{2,1,0:T(8,128)}, u32[]{:S(2)}) copy-start(f32[1,8,128]{2,1,0:T(8,128)} %param.28) | copy-start | bytes 12292
  14.8 21.3 %copy-start.8 = (f32[1,8,128]{2,1,0:T(8,128)S(1)}, f32[1,8,128]{2,1,0:T(8,128)}, u32[]{:S(2)}) copy-start(f32[1,8,128]{2,1,0:T(8,128)} %param.24) | copy-start | bytes 12292
  17.1 143.8 %all-gather.11.cloned.1.call-start = ((), (), s32[]{:S(2)}) async-start(), calls=%async_computation.3 | async-start | bytes 2228224 | tf_op jit(solution)/shard_map/all_gather | solution.py:114
  17.9 185.7 %all-gather.5.cloned.1.call-start = ((), (), s32[]{:S(2)}) async-start(), calls=%async_computation | async-start | bytes 2228224 | tf_op jit(solution)/shard_map/all_gather | solution.py:116
  18.6 227.4 %all-gather.7.cloned.1.call-start = ((), (), s32[]{:S(2)}) async-start(), calls=%async_computation.1 | async-start | bytes 2228224 | tf_op jit(solution)/shard_map/all_gather | solution.py:115
  19.2 269.3 %all-gather.9.cloned.1.call-start = ((), (), s32[]{:S(2)}) async-start(), calls=%async_computation.2 | async-start | bytes 2228224 | tf_op jit(solution)/shard_map/all_gather | solution.py:117
  19.8 387.0 %all-reduce.11.cloned.1.call-start = ((), (), s32[]{:S(2)}) async-start(), calls=%async_computation.5 | async-start | bytes 4194304 | tf_op jit(solution)/shard_map/psum | solution.py:138
  295.0 8.5 %copy-start.6 = (s32[1,64]{1,0:T(1,128)S(1)}, s32[1,64]{1,0:T(1,128)}, u32[]{:S(2)}) copy-start(s32[1,64]{1,0:T(1,128)} %param.16) | copy-start | bytes 772
  295.1 8.5 %copy-start.10 = (f32[1,8,128]{2,1,0:T(8,128)S(1)}, f32[1,8,128]{2,1,0:T(8,128)}, u32[]{:S(2)}) copy-start(f32[1,8,128]{2,1,0:T(8,128)} %param.26) | copy-start | bytes 12292
  295.1 8.8 %copy-start.5 = (f32[1,8,128]{2,1,0:T(8,128)S(1)}, f32[1,8,128]{2,1,0:T(8,128)}, u32[]{:S(2)}) copy-start(f32[1,8,128]{2,1,0:T(8,128)} %param.29) | copy-start | bytes 12292
  295.1 9.0 %copy-start.1 = (f32[1,64,128,128]{3,2,1,0:T(8,128)S(1)}, f32[1,64,128,128]{3,2,1,0:T(8,128)}, u32[]{:S(2)}) copy-start(f32[1,64,128,128]{3,2,1,0:T(8,128)} %param.15) | copy-start | bytes 12582916
  307.7 99.0 %copy-start.3 = (f32[4096,128]{1,0:T(8,128)S(1)}, f32[4096,128]{1,0:T(8,128)}, u32[]{:S(2)}) copy-start(f32[4096,128]{1,0:T(8,128)} %all-gather.11.cloned.1.call-done) | copy-start | bytes 6291460
  310.0 217.4 %all-reduce.13.cloned.1.call-start = ((), (), s32[]{:S(2)}) async-start(), calls=%async_computation.6 | async-start | bytes 4194304 | tf_op jit(solution)/shard_map/psum | solution.py:138
  415.2 9.0 %copy-start.2 = (f32[1,64,128,128]{3,2,1,0:T(8,128)S(1)}, f32[1,64,128,128]{3,2,1,0:T(8,128)}, u32[]{:S(2)}) copy-start(f32[1,64,128,128]{3,2,1,0:T(8,128)} %param.15) | copy-start | bytes 12582916
Sparse Core Ops, SparseCore 0:
  17.2 100.5 all-reduce.8
  120.3 40.6 all-gather.10
  163.3 40.1 all-gather.4
  205.8 40.1 all-gather.6
  248.2 40.1 all-gather.8
  310.2 96.5 all-reduce.10
  430.3 97.0 all-reduce.12
where the time goes:
time: 588 us
  waiting for transfers between devices  407 us (69%)
  blocking collectives  81.2 us (14%)
  matrix products  41.5 us (7%)
  other arithmetic  31.8 us (5%)
  between operations  16.3 us (3%)
  local copies, waits for them, and re-layouts  9.54 us (2%)
    psum x3, waiting for transfers between devices, shards(): grad_first = lax.psum(grad_first_part, ('scen', 'blk', 'sub'))  234 us
    all_gather x1, waiting for transfers between devices, shards(): lax.all_gather(cost_first, ('scen', 'blk', 'sub'), axis=0, tiled=True)  43.1 us
    all_gather x1, waiting for transfers between devices, shards(): lax.all_gather(upper_first, ('scen', 'blk', 'sub'), axis=0, tiled=True)  42.6 us
    all_gather x1, waiting for transfers between devices, shards(): lax.all_gather(lower_first, ('scen', 'blk', 'sub'), axis=0, tiled=True)  42.5 us
    all_gather x1, waiting for transfers between devices, shards(): lax.all_gather(first_start, ('scen', 'blk', 'sub'), axis=0, tiled=True)  42.4 us
    unnamed x3, blocking collectives  34.2 us
    psum x1, blocking collectives, shards(): squares.append(lax.psum(local_square, ('scen', 'blk', 'sub')))  31.1 us
    dot_general x3, matrix products, forward_window(): jnp.einsum('skij,skj->ski', block_matrices, blocks, precision=precise)  25.2 us
  transfers between devices with their start and end apart: 7, of which 7 were waited for; matrix products, arithmetic and copies ran while one was open for 1% of the time, Pallas kernels for 0%

commit v1 on v0

v1 whole, which is shorter than its diff:
```python
import functools

import jax
import jax.numpy as jnp
from jax import lax
from jax.experimental import pallas as pl
from jax.experimental.pallas import tpu as pltpu
from jax.sharding import PartitionSpec as P

ITERS = 3
STEP_PRIMAL = 0.4
STEP_DUAL = 0.4
SHARED = 4
GROUP = ("scen", "blk", "sub")
PAIR = ("blk", "sub")
F32 = jnp.float32
VM = pl.BlockSpec(memory_space=pltpu.VMEM)
SM = pl.BlockSpec(memory_space=pltpu.SMEM)
ACCS = 2


def exact_dot(a, b, contract=(1, 0)):
    dims = (((contract[0],), (contract[1],)), ((), ()))
    return lax.dot_general(a, b, dims, precision=lax.Precision.HIGHEST, preferred_element_type=F32)


def count_dot(a, b):
    return jnp.dot(a, b, preferred_element_type=F32)


def iota(shape, dim):
    return lax.broadcasted_iota(jnp.int32, shape, dim).astype(F32)


def as_float(flags):
    return jnp.where(flags, 1.0, 0.0).astype(F32)


def earlier(size):
    return as_float(iota((size, size), 0) < iota((size, size), 1))


def second_onehot(ids_row, count_first, count_second):
    slots = ids_row.shape[1]
    return as_float(ids_row - float(count_first) == iota((count_second, slots), 0))


def adjoint_products(blocks, rows, spread, parts):
    slots, tile, _ = blocks.shape
    for n in range(slots):
        row = rows[0, n]
        total = None
        for i in range(tile // 8):
            term = blocks[n, pl.ds(i * 8, 8), :] * spread[row, pl.ds(i * 8, 8), :]
            total = term if total is None else total + term
        parts[n] = total
    return jnp.sum(parts[...], axis=1)


def spread_duals(dual_t, spread):
    tile = spread.shape[1]
    for r in range(spread.shape[0]):
        spread[r] = jnp.broadcast_to(dual_t[:, r : r + 1], (tile, tile))


def start_kernel(sizes, blocks, rows, ids, dual, bound, cost2, upper2, second, intensity, carbon,
                 prod_out, sec_out, dual_out, bound_out, spread, parts, square):
    tile, own2, count_first, count_second = sizes
    local_rows = dual.shape[0]
    for source, target in ((dual, dual_out), (bound, bound_out)):
        square[...] = jnp.zeros_like(square)
        square[pl.ds(0, local_rows), :] = source[...]
        target[...] = jnp.transpose(square[...])
    spread_duals(dual_out[...], spread)
    prod = adjoint_products(blocks, rows, spread, parts)
    prod_out[...] = prod
    onehot = second_onehot(ids[...].astype(F32), count_first, count_second)
    sec_out[pl.ds(0, count_second), :] = exact_dot(onehot, prod)
    sec_out[pl.ds(count_second, own2), :] = cost2[...] + intensity[carbon[0]]
    sec_out[pl.ds(count_second + own2, own2), :] = upper2[...]
    sec_out[pl.ds(count_second + 2 * own2, own2), :] = second[...]


def plan_kernel(sizes, everyone, ids, prod, cost, lower, upper, first,
                send_out, pick_out, own_out, sum_out, square, shared):
    devices, slots, shard, count_first, most, keep, me_axes = sizes
    me = lax.axis_index(me_axes).astype(F32)
    base = me * float(shard)
    table = everyone[:, 0, :].astype(F32)
    row = ids[...].astype(F32)
    before = earlier(slots)
    asked = as_float((table >= base) & (table < base + float(shard)))
    rank = count_dot(asked, before)
    slot_number = iota((devices, slots), 1)
    lane = iota((devices, 128), 1)
    id_row = jnp.full((devices, 128), -1.0, F32)
    places = []
    for q in range(most):
        chosen = asked * as_float(rank == float(q))
        has = jnp.sum(chosen, axis=1, keepdims=True)
        place = jnp.sum(chosen * (table - base), axis=1, keepdims=True)
        number = jnp.sum(chosen * slot_number, axis=1, keepdims=True)
        places.append(jnp.where(has > 0.0, place, -1.0))
        id_row = jnp.where(lane == float(q), jnp.where(has > 0.0, number, -1.0), id_row)
    wanted = as_float(jnp.concatenate(places, axis=0) == iota((most * devices, shard), 1))
    for a, source in enumerate((cost, lower, upper, first)):
        answer = exact_dot(wanted, source[...])
        for q in range(most):
            send_out[:, q * 4 + a, :] = answer[q * devices : (q + 1) * devices]
    eye = as_float(iota((slots, slots), 0) == iota((slots, slots), 1))
    column = jnp.sum(eye * row, axis=1, keepdims=True)
    own = as_float(column == row)
    own_out[...] = own
    total = exact_dot(own, prod[...])
    sum_out[...] = total
    again = jnp.max(own * before, axis=0, keepdims=True)
    usable = as_float((row >= 0.0) & (row < float(count_first))) * (1.0 - again)
    square[...] = jnp.full_like(square, -5.0)
    square[pl.ds(0, devices), pl.ds(0, slots)] = table
    turned = jnp.transpose(square[...])
    for e in range(devices):
        named = as_float(turned[:slots, e : e + 1] == row)
        shared[pl.ds(e, 1), :] = jnp.max(named, axis=0, keepdims=True) * usable
    both = shared[...] * as_float(iota((devices, slots), 0) != me)
    count = jnp.max(jnp.sum(both, axis=1, keepdims=True), axis=0, keepdims=True)
    id_row = jnp.where(lane == float(most + keep), as_float(count > float(keep)), id_row)
    rank = count_dot(both, before)
    picks = []
    for p in range(keep):
        chosen = both * as_float(rank == float(p))
        has = jnp.sum(chosen, axis=1, keepdims=True)
        name = jnp.sum(chosen * row, axis=1, keepdims=True)
        id_row = jnp.where(lane == float(most + p), jnp.where(has > 0.0, name, -1.0), id_row)
        picks.append(chosen)
    pick = jnp.concatenate(picks, axis=0)
    pick_out[...] = pick
    rows = exact_dot(pick, total)
    for p in range(keep):
        send_out[:, most * 4 + p, :] = rows[p * devices : (p + 1) * devices]
    send_out[:, most * 4 + keep, :] = id_row


def side_kernel(sizes, everyone, ids, cost, lower, upper, first, base_out, place_out, reply_out):
    devices, slots, shard, most, me_axes = sizes
    base = lax.axis_index(me_axes).astype(F32) * float(shard)
    table = everyone[:, 0, :].astype(F32)
    row = ids[...].astype(F32)
    before = earlier(slots)
    asked = as_float((table >= base) & (table < base + float(shard)))
    rank = count_dot(asked, before)
    places = []
    for q in range(most):
        chosen = asked * as_float(rank == float(q))
        has = jnp.sum(chosen, axis=1, keepdims=True)
        place = jnp.sum(chosen * (table - base), axis=1, keepdims=True)
        places.append(jnp.where(has > 0.0, place, -1.0))
    wanted = as_float(jnp.concatenate(places, axis=0) == iota((most * devices, shard), 1))
    below = as_float(iota((most * devices, most * devices), 0) > iota((most * devices, most * devices), 1))
    wanted = wanted * as_float(count_dot(below, wanted) == 0.0)
    place_out[...] = wanted
    touched = exact_dot(wanted, jnp.ones((most * devices, cost.shape[1]), F32), (0, 0))
    x = first[...]
    for _ in range(ITERS):
        x = jnp.clip(x - STEP_PRIMAL * cost[...], lower[...], upper[...])
    base_out[...] = jnp.where(touched > 0.0, 0.0, x)
    owner = iota((devices, slots), 0) * float(shard)
    held = as_float((row >= owner) & (row < owner + float(shard)))
    rank = count_dot(held, before)
    for q in range(most):
        reply_out[pl.ds(q * devices, devices), :] = held * as_float(rank == float(q))


def step_kernel(sizes, first_step, last_step, direct, *refs):
    devices, slots, count_first, count_second, own2, peers, most, keep, cells = sizes
    refs = list(refs)
    take = lambda: refs.pop(0)
    blocks, rows, ids, dual_t, bound_t = take(), take(), take(), take(), take()
    row = ids[...].astype(F32)
    if first_step:
        answer = take()
        own_sum = None if direct else take()
        gradient = take() if direct else None
        sec_own = take()
        sec_in = [take() for _ in range(len(peers))]
    else:
        x_in, cost_in, lower_in, upper_in, match_in = take(), take(), take(), take(), take()
        y_in, cost2_in, upper2_in = take(), take(), take()
        if direct:
            gradient = take()
        else:
            own_sum, received = take(), take()
        sec_own = take()
        sec_in = [take() for _ in range(len(peers))]
    if not last_step:
        if not direct:
            own_in, pick_in = take(), take()
    else:
        reply_in = take()
        squares_in = [take() for _ in range(ITERS - 1)]
    if first_step:
        cost_out, lower_out, upper_out, match_out, cost2_out, upper2_out = [take() for _ in range(6)]
    if last_step:
        reply_out, y_out, dual_out = take(), take(), take()
    else:
        x_out, y_out, dual_out, square_out, sec_out, sum_out = [take() for _ in range(6)]
        send_out = None if direct else take()
    spread, parts, second_all = take(), take(), take()
    accs = [take() for _ in range(ACCS)]
    square = take()

    if first_step:
        me2 = lax.axis_index(PAIR)
        for k, source in [(0, sec_own)] + list(zip(peers, sec_in)):
            place = pl.multiple_of(lax.bitwise_xor(me2, k) * own2, own2)
            for a in range(3):
                second_all[a, pl.ds(place, own2), :] = source[pl.ds(count_second + a * own2, own2), :]
        cost2, upper2, y = second_all[0], second_all[1], second_all[2]
        cost2_out[...] = cost2
        upper2_out[...] = upper2
        id_row = answer[:, most * 4 + keep, :]
        names = jnp.concatenate([id_row[:, q : q + 1] for q in range(most)], axis=0)
        place = as_float(names == iota((most * devices, slots), 1))
        got = []
        for a in range(4):
            stacked = jnp.concatenate([answer[:, q * 4 + a, :] for q in range(most)], axis=0)
            got.append(exact_dot(place, stacked, (0, 0)))
        cost, lower, upper, x = got
        cost_out[...] = cost
        lower_out[...] = lower
        upper_out[...] = upper
        names = jnp.concatenate([id_row[:, most + p : most + p + 1] for p in range(keep)], axis=0)
        match = as_float(names == row)
        match_out[...] = match
        if not direct:
            fresh = jnp.concatenate([answer[:, most * 4 + p, :] for p in range(keep)], axis=0)
    else:
        x, cost, lower, upper, match = x_in[...], cost_in[...], lower_in[...], upper_in[...], match_in[...]
        y, cost2, upper2 = y_in[...], cost2_in[...], upper2_in[...]
        if not direct:
            fresh = jnp.concatenate([received[:, p, :] for p in range(keep)], axis=0)
    if direct:
        grad = gradient[...]
    else:
        grad = own_sum[...] + exact_dot(match, fresh, (0, 0))
    grad2 = sec_own[pl.ds(0, count_second), :]
    for source in sec_in:
        grad2 = grad2 + source[pl.ds(0, count_second), :]
    x_next = jnp.clip(x - STEP_PRIMAL * (cost - grad), lower, upper)
    y_next = jnp.clip(y - STEP_PRIMAL * (cost2 - grad2), 0.0, upper2)
    onehot = second_onehot(row, count_first, count_second)
    parts[0:slots // 8] = (
        (2.0 * x_next - x) + exact_dot(onehot, 2.0 * y_next - y, (0, 0))
    ).reshape(slots // 8, 8, x.shape[1])
    y_out[...] = y_next
    for acc in accs:
        acc[...] = jnp.zeros_like(acc)
    tile = blocks.shape[1]
    bars = parts[0:slots // 8].reshape(slots, tile)
    for n in range(slots):
        r = rows[0, n]
        acc = accs[n % ACCS]
        bar = jnp.broadcast_to(bars[n : n + 1, :], (8, tile))
        for i in range(tile // 8):
            acc[r, pl.ds(i * 8, 8), :] += blocks[n, pl.ds(i * 8, 8), :] * bar
    local_rows = spread.shape[0]
    duals = dual_t[...]
    bounds = bound_t[...]
    lane = lax.broadcasted_iota(jnp.int32, (tile, tile), 1)
    next_dual = jnp.zeros((tile, tile), F32)
    squares = jnp.zeros((tile, 1), F32)
    for r in range(local_rows):
        total = accs[0][r]
        for acc in accs[1:]:
            total = total + acc[r]
        residual = bounds[:, r : r + 1] - jnp.sum(total, axis=1, keepdims=True)
        squares = squares + residual * residual
        column = jnp.maximum(duals[:, r : r + 1] + STEP_DUAL * residual, 0.0)
        wide = jnp.broadcast_to(column, (tile, tile))
        spread[r] = wide
        next_dual = jnp.where(lane == r, wide, next_dual)
    squares = jnp.broadcast_to(jnp.sum(squares, axis=0, keepdims=True), (1, tile))
    if last_step:
        square[...] = jnp.transpose(next_dual)
        dual_out[...] = square[pl.ds(0, local_rows), :]
        lanes = lax.broadcasted_iota(jnp.int32, (1, tile), 1)
        note = jnp.zeros((1, tile), F32)
        for k, value in enumerate([s[...] for s in squares_in] + [squares]):
            note = jnp.where(lanes == k, value, note)
        reply = exact_dot(reply_in[...], x_next)
        for q in range(most):
            reply_out[:, q, :] = reply[q * devices : (q + 1) * devices]
        reply_out[:, most, :] = jnp.broadcast_to(note, (devices, tile))
    else:
        x_out[...] = x_next
        dual_out[...] = next_dual
        square_out[...] = squares
        prod = adjoint_products(blocks, rows, spread, parts)
        sec_out[...] = exact_dot(onehot, prod)
        if direct:
            sum_out[...] = prod
        else:
            total = exact_dot(own_in[...], prod)
            sum_out[...] = total
            out = exact_dot(pick_in[...], total)
            for p in range(keep):
                send_out[:, p, :] = out[p * devices : (p + 1) * devices]


def finish_kernel(sizes, reply, base, place, first_out, norm_out):
    devices, most, cells = sizes
    rows = jnp.concatenate([reply[:, q, :] for q in range(most)], axis=0)
    first_out[...] = base[...] + exact_dot(place[...], rows, (0, 0))
    norm_out[...] = jnp.sqrt(jnp.sum(reply[:, most, :], axis=0, keepdims=True) / float(cells))


def shards(
    block_matrices,
    slot_row_block,
    tile_column,
    block_count,
    carbon_scenario,
    intensity,
    cost_first,
    lower_first,
    upper_first,
    cost_second,
    upper_second,
    row_bound,
    first_start,
    second_start,
    dual_start,
):
    devices = lax.axis_size(GROUP)
    pairs = lax.axis_size(PAIR)
    scenarios, slots = slot_row_block.shape
    local_rows, tile = row_bound.shape[1:]
    shard = cost_first.shape[0]
    own2 = cost_second.shape[1]
    count_first = shard * devices
    count_second = own2 * pairs
    cells = scenarios * local_rows * tile * devices
    most = -(-scenarios * slots // devices)
    keep = SHARED
    peers = list(range(1, pairs))

    def shape(*dims):
        return jax.ShapeDtypeStruct(dims, F32)

    def scratch(*dims):
        return pltpu.VMEM(dims, F32)

    params = pltpu.CompilerParams(vmem_limit_bytes=40 << 20)

    blocks = block_matrices[0]
    used = jnp.arange(slots, dtype=jnp.int32)[None, :] < block_count
    ids = jnp.where(used, tile_column, -1)
    everyone = lax.all_to_all(
        jnp.broadcast_to(ids[None], (devices, 1, slots)), GROUP, 0, 0, tiled=True
    )
    prod, sec, dual_t, bound_t = pl.pallas_call(
        functools.partial(start_kernel, (tile, own2, count_first, count_second)),
        out_shape=(shape(slots, tile), shape(count_second + 3 * own2, tile), shape(tile, tile), shape(tile, tile)),
        in_specs=[VM, SM, VM, VM, VM, VM, VM, VM, VM, SM],
        scratch_shapes=[scratch(local_rows, tile, tile), scratch(slots, 8, tile), scratch(tile, tile)],
        compiler_params=params,
        name="start",
    )(blocks, slot_row_block, ids, dual_start[0], row_bound[0], cost_second[0], upper_second[0],
      second_start[0], intensity, carbon_scenario)
    firsts = (cost_first, lower_first, upper_first, first_start)
    width = -(-(most * 4 + keep + 1) // 8) * 8
    send, pick, own, own_sum = pl.pallas_call(
        functools.partial(plan_kernel, (devices, slots, shard, count_first, most, keep, GROUP)),
        out_shape=(shape(devices, width, tile), shape(keep * devices, slots), shape(slots, slots), shape(slots, tile)),
        in_specs=[VM] * 7,
        scratch_shapes=[scratch(128, 128), scratch(devices, slots)],
        compiler_params=params,
        name="plan",
    )(everyone, ids, prod, *firsts)
    answer = lax.all_to_all(send, GROUP, 0, 0, tiled=True)
    base, place, reply_pick = pl.pallas_call(
        functools.partial(side_kernel, (devices, slots, shard, most, GROUP)),
        out_shape=(shape(shard, tile), shape(most * devices, shard), shape(most * devices, slots)),
        in_specs=[VM] * 6,
        compiler_params=params,
        name="side",
    )(everyone, ids, *firsts)

    def swap(value):
        return [lax.ppermute(value, PAIR, [(i, i ^ k) for i in range(pairs)]) for k in peers]

    sec_in = swap(sec)
    overflow = jnp.max(answer[:, most * 4 + keep, most + keep]) > 0.5
    step_sizes = (devices, slots, count_first, count_second, own2, peers, most, keep, cells)
    step_scratch = (
        [scratch(local_rows, tile, tile), scratch(slots, 8, tile), scratch(3, count_second, tile)]
        + [scratch(local_rows, tile, tile)] * ACCS
        + [scratch(tile, tile)]
    )
    reply_width = -(-(most + 1) // 8) * 8

    def exchange(value):
        gathered = lax.all_gather(value, GROUP, axis=0, tiled=True)
        match = (everyone.reshape(1, -1) == ids.reshape(-1, 1)).astype(F32)
        return jnp.dot(match, gathered, precision=lax.Precision.HIGHEST)

    def iterate(direct, operands):
        answer, prod, own_sum, sec, dual_t, sec_in = operands
        squares = []
        for step in range(ITERS):
            first_step, last_step = step == 0, step == ITERS - 1
            args = [blocks, slot_row_block, ids, dual_t, bound_t]
            if first_step:
                args.append(answer)
                args.append(exchange(prod) if direct else own_sum)
            else:
                args += [x, cost, lower, upper, match, y, cost2, upper2]
                args += [exchange(own_sum)] if direct else [own_sum, lax.all_to_all(send, GROUP, 0, 0, tiled=True)]
                sec_in = swap(sec)
            args += [sec] + list(sec_in)
            if last_step:
                args += [reply_pick] + squares
                outs = [shape(devices, reply_width, tile), shape(count_second, tile), shape(local_rows, tile)]
            else:
                if not direct:
                    args += [own, pick]
                outs = [shape(slots, tile), shape(count_second, tile), shape(tile, tile), shape(1, tile),
                        shape(count_second, tile), shape(slots, tile)]
                if not direct:
                    outs.append(shape(devices, keep, tile))
            if first_step:
                outs = [shape(slots, tile)] * 3 + [shape(keep * devices, slots)] + [shape(count_second, tile)] * 2 + outs
            results = list(
                pl.pallas_call(
                    functools.partial(step_kernel, step_sizes, first_step, last_step, direct),
                    out_shape=tuple(outs),
                    in_specs=[VM, SM] + [VM] * (len(args) - 2),
                    scratch_shapes=step_scratch,
                    compiler_params=params,
                    name="step",
                )(*args)
            )
            if first_step:
                cost, lower, upper, match, cost2, upper2 = results[:6]
                results = results[6:]
            if last_step:
                reply, y, dual = results
            else:
                x, y, dual_t, square, sec, own_sum = results[:6]
                squares.append(square)
                if not direct:
                    send = results[6]
        return lax.all_to_all(reply, GROUP, 0, 0, tiled=True), y, dual

    reply, y, dual = lax.cond(
        overflow,
        functools.partial(iterate, True),
        functools.partial(iterate, False),
        (answer, prod, own_sum, sec, dual_t, sec_in),
    )
    first_final, norms = pl.pallas_call(
        functools.partial(finish_kernel, (devices, most, cells)),
        out_shape=(shape(shard, tile), shape(1, tile)),
        in_specs=[VM] * 3,
        compiler_params=params,
        name="finish",
    )(reply, base, place)
    second_final = lax.dynamic_slice_in_dim(y, lax.axis_index(PAIR) * own2, own2, 0)
    return first_final, second_final[None], dual[None], norms[0, :ITERS]


def solution(mesh):
    return jax.shard_map(
        shards,
        mesh=mesh,
        in_specs=(
            P(("grp", "scen"), ("blk", "sub"), None, None),
            P(("grp", "scen"), ("blk", "sub")),
            P(("grp", "scen"), ("blk", "sub")),
            P(("grp", "scen"), ("blk", "sub")),
            P(("grp", "scen")),
            P(None, ("blk", "sub"), None),
            P(("grp", "scen", "blk", "sub"), None),
            P(("grp", "scen", "blk", "sub"), None),
            P(("grp", "scen", "blk", "sub"), None),
            P(("grp", "scen"), ("blk", "sub"), None),
            P(("grp", "scen"), ("blk", "sub"), None),
            P(("grp", "scen"), ("blk", "sub"), None),
            P(("grp", "scen", "blk", "sub"), None),
            P(("grp", "scen"), ("blk", "sub"), None),
            P(("grp", "scen"), ("blk", "sub"), None),
        ),
        out_specs=(
            P(("grp", "scen", "blk", "sub"), None),
            P(("grp", "scen"), ("blk", "sub"), None),
            P(("grp", "scen"), ("blk", "sub"), None),
            P("grp"),
        ),
        check_vma=False,
    )
```

time: 588 us -> 84.1 us (0.14)
  waiting for transfers between devices: 407 us -> 15.3 us
  blocking collectives: 81.2 us -> 10.1 us
  matrix products: 41.5 us -> 0 us
  other arithmetic: 31.8 us -> 2.01 us
  starting transfers between devices: 0.27 us -> 26.5 us
  Pallas kernels: 0 us -> 20.5 us
  between operations: 16.3 us -> 2.78 us
    psum x3 -> x0, waiting for transfers between devices: 234 us -> none  [shards(): grad_first = lax.psum(grad_first_part, ('scen', 'blk', 'sub'))]
    all_gather x4 -> x0, waiting for transfers between devices: 171 us -> none  [the longest x1 43.1 us: shards(): lax.all_gather(cost_first, ('scen', 'blk', 'sub'), axis=0, tiled=True)]
    dot_general x13 -> x0, matrix products: 41.5 us -> none  [the longest x3 25.2 us: forward_window(): jnp.einsum('skij,skj->ski', block_matrices, blocks, precision=precise)]
    unnamed x3 -> x0, blocking collectives: 34.2 us -> none
    psum x1 -> x0, blocking collectives: 31.1 us -> none  [shards(): squares.append(lax.psum(local_square, ('scen', 'blk', 'sub')))]
    pallas_call x0 -> x7, Pallas kernels: none -> 20.5 us  [the longest x3 14 us: iterate(): pl.pallas_call(functools.partial(step_kernel, step_sizes, first_step, las...]
    all_to_all x0 -> x4, starting transfers between devices: none -> 20.4 us  [the longest x1 7.36 us: shards(): lax.all_to_all(jnp.broadcast_to(ids[None], (devices, 1, slots)), GROUP, 0...]
    sub x6 -> x0, other arithmetic: 18.9 us -> none  [the longest x3 18.3 us: shards(): first_source = 2.0 * first_next - first_now]
  transfers between devices with their start and end apart: 7 -> 13, of which waited for: 7 -> 7; matrix products, arithmetic and copies ran while one was open for 1% -> 2% of each run, Pallas kernels for 0% -> 5%
where the time goes in v1:
time: 84.1 us; the launch traced here: 83.3 us
  starting transfers between devices  26.5 us (32%)
  Pallas kernels  20.5 us (24%)
  waiting for transfers between devices  15.3 us (18%)
  blocking collectives  10.1 us (12%)
  local copies, waits for them, and re-layouts  6.05 us (7%)
  between operations  2.78 us (3%)
  other arithmetic  2.01 us (2%)
    pallas_call x3, Pallas kernels, iterate(): pl.pallas_call(functools.partial(step_kernel, step_sizes, first_step, las...  14 us
    all_to_all x1, blocking collectives, iterate(): return (lax.all_to_all(reply, GROUP, 0, 0, tiled=True), y, dual)  10.1 us
    all_to_all x1, starting transfers between devices, shards(): lax.all_to_all(jnp.broadcast_to(ids[None], (devices, 1, slots)), GROUP, 0...  7.36 us
    all_to_all x2, starting transfers between devices, iterate(): lax.all_to_all(send, GROUP, 0, 0, tiled=True)  6.99 us
    ppermute x9, waiting for transfers between devices, swap(): lax.ppermute(value, PAIR, [(i, i ^ k) for i in range(pairs)])  6.33 us
    all_to_all x1, waiting for transfers between devices, shards(): answer = lax.all_to_all(send, GROUP, 0, 0, tiled=True)  6.15 us
    ppermute x9, starting transfers between devices, swap(): lax.ppermute(value, PAIR, [(i, i ^ k) for i in range(pairs)])  6.12 us
    all_to_all x1, starting transfers between devices, shards(): answer = lax.all_to_all(send, GROUP, 0, 0, tiled=True)  6.01 us
  transfers between devices with their start and end apart: 13, of which 7 were waited for; matrix products, arithmetic and copies ran while one was open for 2% of the time, Pallas kernels for 5%

profile of v1, /device:TPU:0, one launch (start us, length us, event | category | flops | bytes accessed | tf_op | source)
XLA Modules:
  0.0 83.3 jit_solution(10785362040919294799)
XLA Ops:
  1.4 0.7 fusion.15
  2.6 7.4 %all-to-all-start.4 = ((s32[16,1,64]{2,1,0:T(1,128)}), s32[16,1,64]{2,1,0:T(1,128)S(1)}, u32[]{:S(2)}, u32[]{:S(2)}) async-start(s32[16,1,64]{2,1,0:T(1,128)} %broadcast_in_dim.21), calls=%async_computation.4 | async-start | bytes 16384 | tf_op jit(solution)/shard_map/all_to_all | solution.py:357
  10.0 0.7 compare_select_fusion.ids
  11.3 0.9 %copy-done.4 = f32[24,8,128]{2,1,0:T(8,128)S(1)} copy-done((f32[24,8,128]{2,1,0:T(8,128)S(1)}, f32[24,8,128]{2,1,0:T(8,128)}, u32[]{:S(2)}) %copy-start.4) | copy-done | bytes 98328
  12.2 0.7 copy-done.5
  12.9 0.7 copy-done.6
  13.6 0.7 copy-done.7
  14.3 0.7 copy-done.8
  15.0 0.7 copy-done.9
  15.7 3.1 %start.1 = (f32[64,128]{1,0:T(8,128)S(1)}, f32[56,128]{1,0:T(8,128)S(1)}, f32[128,128]{1,0:T(8,128)S(1)}, f32[128,128]{1,0:T(8,128)S(1)}) custom-call(f32[64,128,128]{2,1,0:T(8,128)} %bitcast.25, s32[1,64]{1,0:T(1,128)} %rows.1, s32[1,64]{1,0:T(1,128)S(1)} %compare_select_fusion.ids, f32[8,128]{1,0:T(8,128)S(1)} %bitcast.20, f32[8,128]{1,0:T(8,128)S(1)} %bitcast.21, ...), custom_call_target="tpu_custom_call" | custom-call | tf_op jit(solution)/shard_map/start/pallas_call | solution.py:360
  18.8 1.7 %plan.1 = (f32[16,24,128]{2,1,0:T(8,128)}, f32[64,64]{1,0:T(8,128)S(1)}, f32[64,64]{1,0:T(8,128)S(1)}, f32[64,128]{1,0:T(8,128)S(1)}) custom-call(s32[16,1,64]{2,1,0:T(1,128)S(1)} %all-to-all-done.4.everyone, s32[1,64]{1,0:T(1,128)S(1)} %compare_select_fusion.ids, f32[64,128]{1,0:T(8,128)S(1)} %get-tuple-element.145.prod, f32[256,128]{1,0:T(8,128)S(1)} %copy-done, ...), custom_call_target="tpu_custom_call" | custom-call | tf_op jit(solution)/shard_map/plan/pallas_call | solution.py:371
  20.5 6.0 %all-to-all-start.5 = ((f32[16,24,128]{2,1,0:T(8,128)}), f32[16,24,128]{2,1,0:T(8,128)S(1)}, u32[]{:S(2)}, u32[]{:S(2)}) async-start(f32[16,24,128]{2,1,0:T(8,128)} %get-tuple-element.146), calls=%async_computation.5 | async-start | bytes 393216 | tf_op jit(solution)/shard_map/all_to_all | solution.py:379
  26.9 1.7 %collective-permute-start.13 = (f32[56,128]{1,0:T(8,128)S(1)}, f32[56,128]{1,0:T(8,128)S(1)}, u32[]{:S(2)}, u32[]{:S(2)}) collective-permute-start(f32[56,128]{1,0:T(8,128)S(1)} %get-tuple-element.150), channel_id=1, source_target_pairs={{0,2},{1,3},{2,0},{3,1},{4,6},{5,7},{6,4},{7,5},{8,10},{9,11},{10,... | collective-permute-start | bytes 86024 | tf_op jit(solution)/shard_map/ppermute | solution.py:389
  28.6 0.7 side.1
  29.4 6.1 %all-to-all-done.5 = f32[16,24,128]{2,1,0:T(8,128)S(1)} async-done(((f32[16,24,128]{2,1,0:T(8,128)}), f32[16,24,128]{2,1,0:T(8,128)S(1)}, u32[]{:S(2)}, u32[]{:S(2)}) %all-to-all-start.5) | async-done | bytes 196640 | tf_op jit(solution)/shard_map/all_to_all | solution.py:379
  35.5 0.7 slice_reduce_fusion
  36.9 44.3 %conditional.1 = (f32[16,8,128]{2,1,0:T(8,128)S(1)}, f32[32,128]{1,0:T(8,128)S(1)}, f32[8,128]{1,0:T(8,128)}) conditional(s32[]{:T(128)} %convert_element_type.2, (f32[64,128,128]{2,1,0:T(8,128)}, s32[1,64]{1,0:T(1,128)S(1)}, s32[1,64]{1,0:T(1,128)S(1)}, f32[128,128]{1,0:T(8,128)S(1)}, f32[128,128]{1,0:T(8,128)S(1)}, ...), branch_computations={%region_1.2_spmd, %region_2.3_spmd} | conditional | flops 302186496 | bytes 20673584 | solution.py:454
  36.9 5.0 %step.6 = (f32[64,128]{1,0:T(8,128)S(1)}, f32[64,128]{1,0:T(8,128)S(1)}, f32[64,128]{1,0:T(8,128)S(1)}, f32[64,64]{1,0:T(8,128)S(1)}, f32[32,128]{1,0:T(8,128)S(...) custom-call(f32[64,128,128]{2,1,0:T(8,128)} %get-tuple-element.54.re, ...), custom_call_target="tpu_custom_call" | custom-call | tf_op jit(solution)/shard_map/cond/branch_0_fun/step/pallas_call | solution.py:433
  41.9 3.5 %all-to-all-start = ((f32[16,4,128]{2,1,0:T(4,128)}), f32[16,4,128]{2,1,0:T(4,128)S(1)}, u32[]{:S(2)}, u32[]{:S(2)}) async-start(f32[16,4,128]{2,1,0:T(4,128)} %get-tuple-element.77), calls=%async_computation | async-start | bytes 65536 | tf_op jit(solution)/shard_map/cond/branch_0_fun/all_to_all | solution.py:417
  45.7 1.7 %collective-permute-start.1 = (f32[32,128]{1,0:T(8,128)S(1)}, f32[32,128]{1,0:T(8,128)S(1)}, u32[]{:S(2)}, u32[]{:S(2)}) collective-permute-start(f32[32,128]{1,0:T(8,128)S(1)} %get-tuple-element.78.refs_15_), channel_id=1, source_target_pairs={{0,2},{1,3},{2,0},{3,1},{4,6},{5,7},{6,4},{7,5},{8,10},{9,11},{10,... | collective-permute-start | bytes 49160 | tf_op jit(solution)/shard_map/cond/branch_0_fun/ppermute | solution.py:389
  47.4 2.1 %collective-permute-done.1.refs_17_ = f32[32,128]{1,0:T(8,128)S(1)} collective-permute-done((f32[32,128]{1,0:T(8,128)S(1)}, f32[32,128]{1,0:T(8,128)S(1)}, u32[]{:S(2)}, u32[]{:S(2)}) %collective-permute-start.1) | collective-permute-done | bytes 16416 | tf_op jit(solution)/shard_map/cond/branch_0_fun/ppermute | solution.py:389
  49.4 1.1 %collective-permute-done.2.refs_18_ = f32[32,128]{1,0:T(8,128)S(1)} collective-permute-done((f32[32,128]{1,0:T(8,128)S(1)}, f32[32,128]{1,0:T(8,128)S(1)}, u32[]{:S(2)}, u32[]{:S(2)}) %collective-permute-start.2) | collective-permute-done | bytes 16416 | tf_op jit(solution)/shard_map/cond/branch_0_fun/ppermute | solution.py:389
  50.6 1.4 %all-to-all-done.refs_14_ = f32[16,4,128]{2,1,0:T(4,128)S(1)} async-done(((f32[16,4,128]{2,1,0:T(4,128)}), f32[16,4,128]{2,1,0:T(4,128)S(1)}, u32[]{:S(2)}, u32[]{:S(2)}) %all-to-all-start) | async-done | bytes 32800 | tf_op jit(solution)/shard_map/cond/branch_0_fun/all_to_all | solution.py:417
  52.0 4.7 %step.7 = (f32[64,128]{1,0:T(8,128)S(1)}, f32[32,128]{1,0:T(8,128)S(1)}, f32[128,128]{1,0:T(8,128)S(1)}, f32[1,128]{1,0:T(1,128)S(1)}, f32[32,128]{1,0:T(8,128)S...) custom-call(f32[64,128,128]{2,1,0:T(8,128)} %get-tuple-element.54.refs_0_, s32[1,64]{1,0:T(1,128)S(1)} %get-tuple-element.55.refs_1_, ...), custom_call_target="tpu_custom_call" | custom-call | tf_op jit(solution)/shard_map/cond/branch_0_fun/step/pallas_call | solution.py:433
  56.7 3.5 %all-to-all-start.1 = ((f32[16,4,128]{2,1,0:T(4,128)}), f32[16,4,128]{2,1,0:T(4,128)S(1)}, u32[]{:S(2)}, u32[]{:S(2)}) async-start(f32[16,4,128]{2,1,0:T(4,128)} %get-tuple-element.83), calls=%async_computation.1 | async-start | bytes 65536 | tf_op jit(solution)/shard_map/cond/branch_0_fun/all_to_all | solution.py:417
  60.6 1.7 %collective-permute-start.4 = (f32[32,128]{1,0:T(8,128)S(1)}, f32[32,128]{1,0:T(8,128)S(1)}, u32[]{:S(2)}, u32[]{:S(2)}) collective-permute-start(f32[32,128]{1,0:T(8,128)S(1)} %get-tuple-element.84.refs_15_), channel_id=1, source_target_pairs={{0,2},{1,3},{2,0},{3,1},{4,6},{5,7},{6,4},{7,5},{8,10},{9,11},{10,... | collective-permute-start | bytes 49160 | tf_op jit(solution)/shard_map/cond/branch_0_fun/ppermute | solution.py:389
  62.3 2.1 %collective-permute-done.4.refs_17_ = f32[32,128]{1,0:T(8,128)S(1)} collective-permute-done((f32[32,128]{1,0:T(8,128)S(1)}, f32[32,128]{1,0:T(8,128)S(1)}, u32[]{:S(2)}, u32[]{:S(2)}) %collective-permute-start.4) | collective-permute-done | bytes 16416 | tf_op jit(solution)/shard_map/cond/branch_0_fun/ppermute | solution.py:389
  64.4 1.1 %collective-permute-done.5.refs_18_ = f32[32,128]{1,0:T(8,128)S(1)} collective-permute-done((f32[32,128]{1,0:T(8,128)S(1)}, f32[32,128]{1,0:T(8,128)S(1)}, u32[]{:S(2)}, u32[]{:S(2)}) %collective-permute-start.5) | collective-permute-done | bytes 16416 | tf_op jit(solution)/shard_map/cond/branch_0_fun/ppermute | solution.py:389
  65.5 1.4 %all-to-all-done.1.refs_14_ = f32[16,4,128]{2,1,0:T(4,128)S(1)} async-done(((f32[16,4,128]{2,1,0:T(4,128)}), f32[16,4,128]{2,1,0:T(4,128)S(1)}, u32[]{:S(2)}, u32[]{:S(2)}) %all-to-all-start.1) | async-done | bytes 32800 | tf_op jit(solution)/shard_map/cond/branch_0_fun/all_to_all | solution.py:417
  66.8 4.2 %step.8 = (f32[16,8,128]{2,1,0:T(8,128)S(1)}, f32[32,128]{1,0:T(8,128)S(1)}, f32[8,128]{1,0:T(8,128)}) custom-call(f32[64,128,128]{2,1,0:T(8,128)} %get-tuple-element.54.refs_0_, s32[1,64]{1,0:T(1,128)S(1)} %get-tuple-element.55.refs_1_, s32[1,64]{1,0:T(1,128)S(1)} %get-tuple-element.56.refs_2_, f32[128,128]{1,0:T(8,128)S(1)} %get-tuple-element.79.refs_3_, ...), custom_call_target="tpu_custom_call" | custom-call | tf_op jit(solution)/shard_map/cond/branch_0_fun/step/pallas_call | solution.py:433
  71.1 10.1 %all_to_all.26 = f32[16,8,128]{2,1,0:T(8,128)S(1)} all-to-all(f32[16,8,128]{2,1,0:T(8,128)S(1)} %get-tuple-element.88), channel_id=1, replica_groups=mesh['grp'=2,'scen'=4,'blk'=2,'sub'=2] {'scen','blk','sub'}, dimensions={0} | all-to-all | bytes 131072 | tf_op jit(solution)/shard_map/cond/branch_0_fun/all_to_all | solution.py:452
  81.2 1.0 %finish.1 = (f32[256,128]{1,0:T(8,128)}, f32[1,128]{1,0:T(1,128)S(1)}) custom-call(f32[16,8,128]{2,1,0:T(8,128)S(1)} %get-tuple-element.154.reply, f32[256,128]{1,0:T(8,128)S(1)} %get-tuple-element.155.base, f32[64,256]{1,0:T(8,128)S(1)} %get-tuple-element.156.place), custom_call_target="tpu_custom_call" | custom-call | tf_op jit(solution)/shard_map/finish/pallas_call | solution.py:460
  (31 shorter events, 2.8 us)
Async XLA Ops:
  0.6 18.1 %copy-start = (f32[256,128]{1,0:T(8,128)S(1)}, f32[256,128]{1,0:T(8,128)}, u32[]{:S(2)}) copy-start(f32[256,128]{1,0:T(8,128)} %cost.3) | copy-start | bytes 393220
  0.6 18.1 %copy-start.1 = (f32[256,128]{1,0:T(8,128)S(1)}, f32[256,128]{1,0:T(8,128)}, u32[]{:S(2)}) copy-start(f32[256,128]{1,0:T(8,128)} %lower.3) | copy-start | bytes 393220
  0.7 18.1 %copy-start.2 = (f32[256,128]{1,0:T(8,128)S(1)}, f32[256,128]{1,0:T(8,128)}, u32[]{:S(2)}) copy-start(f32[256,128]{1,0:T(8,128)} %upper.3) | copy-start | bytes 393220
  0.7 18.1 %copy-start.3 = (f32[256,128]{1,0:T(8,128)S(1)}, f32[256,128]{1,0:T(8,128)}, u32[]{:S(2)}) copy-start(f32[256,128]{1,0:T(8,128)} %first.3) | copy-start | bytes 393220
  2.6 16.1 %all-to-all-start.4 = ((s32[16,1,64]{2,1,0:T(1,128)}), s32[16,1,64]{2,1,0:T(1,128)S(1)}, u32[]{:S(2)}, u32[]{:S(2)}) async-start(s32[16,1,64]{2,1,0:T(1,128)} %broadcast_in_dim.21), calls=%async_computation.4 | async-start | bytes 16384 | tf_op jit(solution)/shard_map/all_to_all | solution.py:357
  11.3 0.9 %copy-start.4 = (f32[24,8,128]{2,1,0:T(8,128)S(1)}, f32[24,8,128]{2,1,0:T(8,128)}, u32[]{:S(2)}) copy-start(f32[24,8,128]{2,1,0:T(8,128)} %intensity.1) | copy-start | bytes 294916
  12.2 0.7 copy-start.5
  12.9 0.7 copy-start.6
  13.6 0.7 copy-start.7
  14.3 0.7 copy-start.8
  15.0 0.7 copy-start.9
  15.7 21.3 %copy-start.11 = (s32[1,64]{1,0:T(1,128)S(1)}, s32[1,64]{1,0:T(1,128)}, u32[]{:S(2)}) copy-start(s32[1,64]{1,0:T(1,128)} %rows.1) | copy-start | bytes 772
  20.5 15.0 %all-to-all-start.5 = ((f32[16,24,128]{2,1,0:T(8,128)}), f32[16,24,128]{2,1,0:T(8,128)S(1)}, u32[]{:S(2)}, u32[]{:S(2)}) async-start(f32[16,24,128]{2,1,0:T(8,128)} %get-tuple-element.146), calls=%async_computation.5 | async-start | bytes 393216 | tf_op jit(solution)/shard_map/all_to_all | solution.py:379
  26.5 10.3 %collective-permute-start.12 = (f32[56,128]{1,0:T(8,128)S(1)}, f32[56,128]{1,0:T(8,128)S(1)}, u32[]{:S(2)}, u32[]{:S(2)}) collective-permute-start(f32[56,128]{1,0:T(8,128)S(1)} %get-tuple-element.150), channel_id=1, source_target_pairs={{0,1},{1,0},{2,3},{3,2},{4,5},{5,4},{6,7},{7,6},{8,9},{9,8},{10,11... | collective-permute-start | bytes 86024 | tf_op jit(solution)/shard_map/ppermute | solution.py:389
  26.9 9.9 %collective-permute-start.13 = (f32[56,128]{1,0:T(8,128)S(1)}, f32[56,128]{1,0:T(8,128)S(1)}, u32[]{:S(2)}, u32[]{:S(2)}) collective-permute-start(f32[56,128]{1,0:T(8,128)S(1)} %get-tuple-element.150), channel_id=1, source_target_pairs={{0,2},{1,3},{2,0},{3,1},{4,6},{5,7},{6,4},{7,5},{8,10},{9,11},{10,... | collective-permute-start | bytes 86024 | tf_op jit(solution)/shard_map/ppermute | solution.py:389
  28.6 8.3 %collective-permute-start.14 = (f32[56,128]{1,0:T(8,128)S(1)}, f32[56,128]{1,0:T(8,128)S(1)}, u32[]{:S(2)}, u32[]{:S(2)}) collective-permute-start(f32[56,128]{1,0:T(8,128)S(1)} %get-tuple-element.150), channel_id=1, source_target_pairs={{0,3},{1,2},{2,1},{3,0},{4,7},{5,6},{6,5},{7,4},{8,11},{9,10},{10,... | collective-permute-start | bytes 86024 | tf_op jit(solution)/shard_map/ppermute | solution.py:389
  41.9 10.1 %all-to-all-start = ((f32[16,4,128]{2,1,0:T(4,128)}), f32[16,4,128]{2,1,0:T(4,128)S(1)}, u32[]{:S(2)}, u32[]{:S(2)}) async-start(f32[16,4,128]{2,1,0:T(4,128)} %get-tuple-element.77), calls=%async_computation | async-start | bytes 65536 | tf_op jit(solution)/shard_map/cond/branch_0_fun/all_to_all | solution.py:417
  45.4 2.0 %collective-permute-start = (f32[32,128]{1,0:T(8,128)S(1)}, f32[32,128]{1,0:T(8,128)S(1)}, u32[]{:S(2)}, u32[]{:S(2)}) collective-permute-start(f32[32,128]{1,0:T(8,128)S(1)} %get-tuple-element.78.refs_15_), channel_id=1, source_target_pairs={{0,1},{1,0},{2,3},{3,2},{4,5},{5,4},{6,7},{7,6},{8,9},{9,8},{10,11... | collective-permute-start | bytes 49160 | tf_op jit(solution)/shard_map/cond/branch_0_fun/ppermute | solution.py:389
  45.7 3.8 %collective-permute-start.1 = (f32[32,128]{1,0:T(8,128)S(1)}, f32[32,128]{1,0:T(8,128)S(1)}, u32[]{:S(2)}, u32[]{:S(2)}) collective-permute-start(f32[32,128]{1,0:T(8,128)S(1)} %get-tuple-element.78.refs_15_), channel_id=1, source_target_pairs={{0,2},{1,3},{2,0},{3,1},{4,6},{5,7},{6,4},{7,5},{8,10},{9,11},{10,... | collective-permute-start | bytes 49160 | tf_op jit(solution)/shard_map/cond/branch_0_fun/ppermute | solution.py:389
  47.4 3.2 %collective-permute-start.2 = (f32[32,128]{1,0:T(8,128)S(1)}, f32[32,128]{1,0:T(8,128)S(1)}, u32[]{:S(2)}, u32[]{:S(2)}) collective-permute-start(f32[32,128]{1,0:T(8,128)S(1)} %get-tuple-element.78.refs_15_), channel_id=1, source_target_pairs={{0,3},{1,2},{2,1},{3,0},{4,7},{5,6},{6,5},{7,4},{8,11},{9,10},{10,... | collective-permute-start | bytes 49160 | tf_op jit(solution)/shard_map/cond/branch_0_fun/ppermute | solution.py:389
  56.7 10.1 %all-to-all-start.1 = ((f32[16,4,128]{2,1,0:T(4,128)}), f32[16,4,128]{2,1,0:T(4,128)S(1)}, u32[]{:S(2)}, u32[]{:S(2)}) async-start(f32[16,4,128]{2,1,0:T(4,128)} %get-tuple-element.83), calls=%async_computation.1 | async-start | bytes 65536 | tf_op jit(solution)/shard_map/cond/branch_0_fun/all_to_all | solution.py:417
  60.3 2.0 %collective-permute-start.3 = (f32[32,128]{1,0:T(8,128)S(1)}, f32[32,128]{1,0:T(8,128)S(1)}, u32[]{:S(2)}, u32[]{:S(2)}) collective-permute-start(f32[32,128]{1,0:T(8,128)S(1)} %get-tuple-element.84.refs_15_), channel_id=1, source_target_pairs={{0,1},{1,0},{2,3},{3,2},{4,5},{5,4},{6,7},{7,6},{8,9},{9,8},{10,11... | collective-permute-start | bytes 49160 | tf_op jit(solution)/shard_map/cond/branch_0_fun/ppermute | solution.py:389
  60.6 3.8 %collective-permute-start.4 = (f32[32,128]{1,0:T(8,128)S(1)}, f32[32,128]{1,0:T(8,128)S(1)}, u32[]{:S(2)}, u32[]{:S(2)}) collective-permute-start(f32[32,128]{1,0:T(8,128)S(1)} %get-tuple-element.84.refs_15_), channel_id=1, source_target_pairs={{0,2},{1,3},{2,0},{3,1},{4,6},{5,7},{6,4},{7,5},{8,10},{9,11},{10,... | collective-permute-start | bytes 49160 | tf_op jit(solution)/shard_map/cond/branch_0_fun/ppermute | solution.py:389
  62.3 3.2 %collective-permute-start.5 = (f32[32,128]{1,0:T(8,128)S(1)}, f32[32,128]{1,0:T(8,128)S(1)}, u32[]{:S(2)}, u32[]{:S(2)}) collective-permute-start(f32[32,128]{1,0:T(8,128)S(1)} %get-tuple-element.84.refs_15_), channel_id=1, source_target_pairs={{0,3},{1,2},{2,1},{3,0},{4,7},{5,6},{6,5},{7,4},{8,11},{9,10},{10,... | collective-permute-start | bytes 49160 | tf_op jit(solution)/shard_map/cond/branch_0_fun/ppermute | solution.py:389

commit v2 on v1

v2 whole, which is shorter than its diff:
```python
import functools

import jax
import jax.numpy as jnp
from jax import lax
from jax.experimental import pallas as pl
from jax.experimental.pallas import tpu as pltpu
from jax.sharding import PartitionSpec as P

ITERS = 3
STEP_PRIMAL = 0.4
STEP_DUAL = 0.4
SHARED = 4
GROUP = ("scen", "blk", "sub")
PAIR = ("blk", "sub")
F32 = jnp.float32
VM = pl.BlockSpec(memory_space=pltpu.VMEM)
SM = pl.BlockSpec(memory_space=pltpu.SMEM)
HB = pl.BlockSpec(memory_space=pl.ANY)
ACCS = 2
CHUNK = 16


def exact_dot(a, b, contract=(1, 0)):
    dims = (((contract[0],), (contract[1],)), ((), ()))
    return lax.dot_general(a, b, dims, precision=lax.Precision.HIGHEST, preferred_element_type=F32)


def count_dot(a, b):
    return jnp.dot(a, b, preferred_element_type=F32)


def iota(shape, dim):
    return lax.broadcasted_iota(jnp.int32, shape, dim).astype(F32)


def as_float(flags):
    return jnp.where(flags, 1.0, 0.0).astype(F32)


def earlier(size):
    return as_float(iota((size, size), 0) < iota((size, size), 1))


def second_onehot(ids_row, count_first, count_second):
    slots = ids_row.shape[1]
    return as_float(ids_row - float(count_first) == iota((count_second, slots), 0))


def fetch_blocks(source, target, sems):
    copies = [
        pltpu.make_async_copy(source.at[pl.ds(k, CHUNK)], target.at[pl.ds(k, CHUNK)], sems.at[k // CHUNK])
        for k in range(0, target.shape[0], CHUNK)
    ]
    for copy in copies:
        copy.start()

    def wait(n):
        if n % CHUNK == 0:
            copies[n // CHUNK].wait()

    return wait


def adjoint_products(kept, rows, spread, parts):
    slots, tile, _ = kept.shape
    for n in range(slots):
        row = rows[0, n]
        total = None
        for i in range(tile // 16):
            part = pl.ds(i * 16, 16)
            term = kept[n, part, :].astype(F32) * spread[row, part, :]
            total = term if total is None else total + term
        parts[n] = total[:8] + total[8:]
    return jnp.sum(parts[...], axis=1)


def spread_duals(dual_t, spread):
    tile = spread.shape[1]
    for r in range(spread.shape[0]):
        spread[r] = jnp.broadcast_to(dual_t[:, r : r + 1], (tile, tile))


def start_kernel(sizes, blocks_in, rows, used, columns, dual, bound, cost2, upper2, second, intensity, carbon,
                 ids_out, prod_out, sec_out, dual_out, bound_out, own_out, sum_out, usable_out,
                 spread, parts, squares, prices, blocks, sems, block_sems):
    tile, own2, count_first, count_second = sizes
    slots = blocks.shape[0]
    local_rows = dual.shape[0]
    places = [sec_out.at[pl.ds(count_second + a * own2, own2), :] for a in range(3)]
    copies = [
        pltpu.make_async_copy(source, target, sems.at[k])
        for k, (source, target) in enumerate([
            (dual, squares.at[0, pl.ds(0, local_rows), :]),
            (bound, squares.at[1, pl.ds(0, local_rows), :]),
            (cost2, places[0]),
            (upper2, places[1]),
            (second, places[2]),
            (intensity.at[carbon[0]], prices),
        ])
    ]
    for copy in copies:
        copy.start()
    wait = fetch_blocks(blocks_in, blocks, block_sems)
    row = columns[...].astype(F32)
    ids_out[...] = row
    active = as_float(iota((slots, tile), 0) < used[0, 0].astype(F32))
    eye = as_float(iota((slots, slots), 0) == iota((slots, slots), 1))
    column = jnp.sum(eye * row, axis=1, keepdims=True)
    own = as_float(column == row)
    own_out[...] = own
    again = jnp.max(own * earlier(slots), axis=0, keepdims=True)
    some = jnp.max(own * active[:, :1], axis=0, keepdims=True)
    usable_out[...] = as_float(row < float(count_first)) * (1.0 - again) * some
    for k in range(2):
        squares[k, pl.ds(local_rows, tile - local_rows), :] = jnp.zeros((tile - local_rows, tile), F32)
    for copy in copies:
        copy.wait()
    for k, target in enumerate((dual_out, bound_out)):
        target[...] = jnp.transpose(squares[k])
    spread_duals(dual_out[...], spread)
    for n in range(slots):
        wait(n)
        r = rows[0, n]
        total = None
        for i in range(tile // 8):
            term = blocks[n, pl.ds(i * 8, 8), :] * spread[r, pl.ds(i * 8, 8), :]
            total = term if total is None else total + term
        parts[n] = total
    prod = jnp.sum(parts[...], axis=1) * active
    prod_out[...] = prod
    onehot = second_onehot(row, count_first, count_second)
    sums = exact_dot(jnp.concatenate([own, onehot], axis=0), prod)
    sum_out[...] = sums[:slots]
    sec_out[pl.ds(0, count_second), :] = sums[slots:]
    sec_out[pl.ds(count_second, own2), :] += prices[...]


def plan_kernel(sizes, everyone, ids, usable, total, cost, lower, upper, first,
                send_out, pick_out, square, shared):
    devices, slots, shard, most, keep, me_axes = sizes
    me = lax.axis_index(me_axes).astype(F32)
    base = me * float(shard)
    table = everyone[:, 0, :].astype(F32)
    row = ids[...]
    before = earlier(slots)
    asked = as_float((table >= base) & (table < base + float(shard)))
    rank = count_dot(asked, before)
    slot_number = iota((devices, slots), 1)
    lane = iota((devices, 128), 1)
    id_row = jnp.full((devices, 128), -1.0, F32)
    places = []
    for q in range(most):
        chosen = asked * as_float(rank == float(q))
        has = jnp.sum(chosen, axis=1, keepdims=True)
        place = jnp.sum(chosen * (table - base), axis=1, keepdims=True)
        number = jnp.sum(chosen * slot_number, axis=1, keepdims=True)
        places.append(jnp.where(has > 0.0, place, -1.0))
        id_row = jnp.where(lane == float(q), jnp.where(has > 0.0, number, -1.0), id_row)
    wanted = as_float(jnp.concatenate(places, axis=0) == iota((most * devices, shard), 1))
    for a, source in enumerate((cost, lower, upper, first)):
        answer = exact_dot(wanted, source[...])
        for q in range(most):
            send_out[:, q * 4 + a, :] = answer[q * devices : (q + 1) * devices]
    square[...] = jnp.full_like(square, -5.0)
    square[pl.ds(0, devices), pl.ds(0, slots)] = table
    turned = jnp.transpose(square[...])
    for e in range(devices):
        named = as_float(turned[:slots, e : e + 1] == row)
        shared[pl.ds(e, 1), :] = jnp.max(named, axis=0, keepdims=True) * usable[...]
    both = shared[...] * as_float(iota((devices, slots), 0) != me)
    count = jnp.max(jnp.sum(both, axis=1, keepdims=True), axis=0, keepdims=True)
    id_row = jnp.where(lane == float(most + keep), as_float(count > float(keep)), id_row)
    rank = count_dot(both, before)
    picks = []
    for p in range(keep):
        chosen = both * as_float(rank == float(p))
        has = jnp.sum(chosen, axis=1, keepdims=True)
        name = jnp.sum(chosen * row, axis=1, keepdims=True)
        id_row = jnp.where(lane == float(most + p), jnp.where(has > 0.0, name, -1.0), id_row)
        picks.append(chosen)
    pick = jnp.concatenate(picks, axis=0)
    pick_out[...] = pick
    rows = exact_dot(pick, total[...])
    for p in range(keep):
        send_out[:, most * 4 + p, :] = rows[p * devices : (p + 1) * devices]
    send_out[:, most * 4 + keep, :] = id_row


def side_kernel(sizes, everyone, ids, own, pick, cost, lower, upper, first, blocks_in, used,
                base_out, place_out, reply_out, stack_out, kept_out, scale_out, tops, blocks, block_sems):
    devices, slots, shard, most, me_axes = sizes
    wait = fetch_blocks(blocks_in, blocks, block_sems)
    base = lax.axis_index(me_axes).astype(F32) * float(shard)
    table = everyone[:, 0, :].astype(F32)
    row = ids[...]
    before = earlier(slots)
    asked = as_float((table >= base) & (table < base + float(shard)))
    rank = count_dot(asked, before)
    places = []
    for q in range(most):
        chosen = asked * as_float(rank == float(q))
        has = jnp.sum(chosen, axis=1, keepdims=True)
        place = jnp.sum(chosen * (table - base), axis=1, keepdims=True)
        places.append(jnp.where(has > 0.0, place, -1.0))
    wanted = as_float(jnp.concatenate(places, axis=0) == iota((most * devices, shard), 1))
    below = as_float(iota((most * devices, most * devices), 0) > iota((most * devices, most * devices), 1))
    wanted = wanted * as_float(count_dot(below, wanted) == 0.0)
    place_out[...] = wanted
    touched = exact_dot(wanted, jnp.ones((most * devices, cost.shape[1]), F32), (0, 0))
    x = first[...]
    for _ in range(ITERS):
        x = jnp.clip(x - STEP_PRIMAL * cost[...], lower[...], upper[...])
    base_out[...] = jnp.where(touched > 0.0, 0.0, x)
    owner = iota((devices, slots), 0) * float(shard)
    held = as_float((row >= owner) & (row < owner + float(shard)))
    rank = count_dot(held, before)
    for q in range(most):
        reply_out[pl.ds(q * devices, devices), :] = held * as_float(rank == float(q))
    stack_out[pl.ds(0, slots), :] = own[...]
    stack_out[pl.ds(slots, pick.shape[0]), :] = count_dot(pick[...], own[...])
    tile = blocks.shape[1]
    for n in range(slots):
        wait(n)
        top = None
        for i in range(tile // 8):
            size = jnp.abs(blocks[n, pl.ds(i * 8, 8), :])
            top = size if top is None else jnp.maximum(top, size)
        tops[n] = top
    top = jnp.max(jnp.max(tops[...], axis=1), axis=1, keepdims=True)
    factors = jnp.broadcast_to(jnp.where(top > 1e-30, 32767.0 / jnp.maximum(top, 1e-30), 0.0), (slots, tile))
    active = as_float(iota((slots, tile), 0) < used[0, 0].astype(F32))
    scale_out[...] = jnp.broadcast_to(top, (slots, tile)) * (1.0 / 32767.0) * active
    for n in range(slots):
        factor = jnp.broadcast_to(factors[n : n + 1, :], (16, tile))
        for i in range(tile // 16):
            part = pl.ds(i * 16, 16)
            level = jnp.floor(blocks[n, part, :] * factor + 0.5)
            kept_out[n, part, :] = level.astype(jnp.int32).astype(jnp.int16)


def step_kernel(sizes, first_step, last_step, direct, *refs):
    devices, slots, count_first, count_second, own2, peers, most, keep, cells = sizes
    refs = list(refs)
    take = lambda: refs.pop(0)
    kept, scale, rows, ids, dual_t, bound_t = [take() for _ in range(6)]
    row = ids[...]
    if first_step:
        answer = take()
        own_sum = None if direct else take()
        gradient = take() if direct else None
        sec_own = take()
        sec_in = [take() for _ in range(len(peers))]
    else:
        x_in, cost_in, lower_in, upper_in, match_in = take(), take(), take(), take(), take()
        y_in, cost2_in, upper2_in = take(), take(), take()
        if direct:
            gradient = take()
        else:
            own_sum, received = take(), take()
        sec_own = take()
        sec_in = [take() for _ in range(len(peers))]
    if not last_step:
        if not direct:
            stack_in = take()
    else:
        reply_in = take()
        squares_in = [take() for _ in range(ITERS - 1)]
    if first_step:
        cost_out, lower_out, upper_out, match_out, cost2_out, upper2_out = [take() for _ in range(6)]
        flag_out = None if direct else take()
    if last_step:
        reply_out, y_out, dual_out = take(), take(), take()
    else:
        x_out, y_out, dual_out, square_out, sec_out, sum_out = [take() for _ in range(6)]
        send_out = None if direct else take()
    spread, parts, second_all = take(), take(), take()
    accs = [take() for _ in range(ACCS)]
    square = take()

    if first_step:
        me2 = lax.axis_index(PAIR)
        for k, source in [(0, sec_own)] + list(zip(peers, sec_in)):
            place = pl.multiple_of(lax.bitwise_xor(me2, k) * own2, own2)
            for a in range(3):
                second_all[a, pl.ds(place, own2), :] = source[pl.ds(count_second + a * own2, own2), :]
        cost2, upper2, y = second_all[0], second_all[1], second_all[2]
        cost2_out[...] = cost2
        upper2_out[...] = upper2
        id_row = answer[:, most * 4 + keep, :]
        names = jnp.concatenate([id_row[:, q : q + 1] for q in range(most)], axis=0)
        place = as_float(names == iota((most * devices, slots), 1))
        got = []
        for a in range(4):
            stacked = jnp.concatenate([answer[:, q * 4 + a, :] for q in range(most)], axis=0)
            got.append(exact_dot(place, stacked, (0, 0)))
        cost, lower, upper, x = got
        cost_out[...] = cost
        lower_out[...] = lower
        upper_out[...] = upper
        names = jnp.concatenate([id_row[:, most + p : most + p + 1] for p in range(keep)], axis=0)
        match = as_float(names == row)
        match_out[...] = match
        if not direct:
            flag_out[0, 0] = jnp.where(jnp.max(id_row[:, most + keep : most + keep + 1]) > 0.5, 1, 0)
            fresh = jnp.concatenate([answer[:, most * 4 + p, :] for p in range(keep)], axis=0)
    else:
        x, cost, lower, upper, match = x_in[...], cost_in[...], lower_in[...], upper_in[...], match_in[...]
        y, cost2, upper2 = y_in[...], cost2_in[...], upper2_in[...]
        if not direct:
            fresh = jnp.concatenate([received[:, p, :] for p in range(keep)], axis=0)
    if direct:
        grad = gradient[...]
    else:
        grad = own_sum[...] + exact_dot(match, fresh, (0, 0))
    grad2 = sec_own[pl.ds(0, count_second), :]
    for source in sec_in:
        grad2 = grad2 + source[pl.ds(0, count_second), :]
    x_next = jnp.clip(x - STEP_PRIMAL * (cost - grad), lower, upper)
    y_next = jnp.clip(y - STEP_PRIMAL * (cost2 - grad2), 0.0, upper2)
    onehot = second_onehot(row, count_first, count_second)
    bars = ((2.0 * x_next - x) + exact_dot(onehot, 2.0 * y_next - y, (0, 0))) * scale[...]
    if last_step:
        parts_y = second_all.at[0]
        parts_y[...] = y_next
        y_out[0] = parts_y[pl.ds(pl.multiple_of(lax.axis_index(PAIR) * own2, own2), own2), :]
    else:
        y_out[...] = y_next
    for acc in accs:
        acc[...] = jnp.zeros_like(acc)
    tile = kept.shape[1]
    for n in range(slots):
        r = rows[0, n]
        acc = accs[n % ACCS]
        bar = jnp.broadcast_to(bars[n : n + 1, :], (16, tile))
        for i in range(tile // 16):
            part = pl.ds(i * 16, 16)
            acc[r, part, :] += kept[n, part, :].astype(F32) * bar
    local_rows = spread.shape[0]
    duals = dual_t[...]
    bounds = bound_t[...]
    lane = lax.broadcasted_iota(jnp.int32, (tile, tile), 1)
    next_dual = jnp.zeros((tile, tile), F32)
    squares = jnp.zeros((tile, 1), F32)
    for r in range(local_rows):
        total = accs[0][r]
        for acc in accs[1:]:
            total = total + acc[r]
        residual = bounds[:, r : r + 1] - jnp.sum(total, axis=1, keepdims=True)
        squares = squares + residual * residual
        column = jnp.maximum(duals[:, r : r + 1] + STEP_DUAL * residual, 0.0)
        wide = jnp.broadcast_to(column, (tile, tile))
        spread[r] = wide
        next_dual = jnp.where(lane == r, wide, next_dual)
    squares = jnp.broadcast_to(jnp.sum(squares, axis=0, keepdims=True), (1, tile))
    if last_step:
        square[...] = jnp.transpose(next_dual)
        dual_out[0] = square[pl.ds(0, local_rows), :]
        lanes = lax.broadcasted_iota(jnp.int32, (1, tile), 1)
        note = jnp.zeros((1, tile), F32)
        for k, value in enumerate([s[...] for s in squares_in] + [squares]):
            note = jnp.where(lanes == k, value, note)
        reply = exact_dot(reply_in[...], x_next)
        for q in range(most):
            reply_out[:, q, :] = reply[q * devices : (q + 1) * devices]
        reply_out[:, most, :] = jnp.broadcast_to(note, (devices, tile))
    else:
        x_out[...] = x_next
        dual_out[...] = next_dual
        square_out[...] = squares
        prod = adjoint_products(kept, rows, spread, parts) * scale[...]
        if direct:
            sec_out[...] = exact_dot(onehot, prod)
            sum_out[...] = prod
        else:
            out = exact_dot(jnp.concatenate([stack_in[...], onehot], axis=0), prod)
            sum_out[...] = out[:slots]
            for p in range(keep):
                send_out[:, p, :] = out[slots + p * devices : slots + (p + 1) * devices]
            sec_out[...] = out[slots + keep * devices :]


def finish_kernel(sizes, reply, base, place, first_out, norm_out):
    devices, most, cells = sizes
    rows = jnp.concatenate([reply[:, q, :] for q in range(most)], axis=0)
    first_out[...] = base[...] + exact_dot(place[...], rows, (0, 0))
    norms = jnp.sqrt(jnp.sum(reply[:, most, :], axis=0, keepdims=True) / float(cells))
    lane = lax.broadcasted_iota(jnp.int32, norms.shape, 1)
    for k in range(ITERS):
        norm_out[k] = jnp.max(jnp.where(lane == k, norms, 0.0))


def shards(
    block_matrices,
    slot_row_block,
    tile_column,
    block_count,
    carbon_scenario,
    intensity,
    cost_first,
    lower_first,
    upper_first,
    cost_second,
    upper_second,
    row_bound,
    first_start,
    second_start,
    dual_start,
):
    devices = lax.axis_size(GROUP)
    pairs = lax.axis_size(PAIR)
    scenarios, slots = slot_row_block.shape
    local_rows, tile = row_bound.shape[1:]
    shard = cost_first.shape[0]
    own2 = cost_second.shape[1]
    count_first = shard * devices
    count_second = own2 * pairs
    cells = scenarios * local_rows * tile * devices
    most = -(-scenarios * slots // devices)
    keep = SHARED
    peers = list(range(1, pairs))

    def shape(*dims):
        return jax.ShapeDtypeStruct(dims, F32)

    def scratch(*dims):
        return pltpu.VMEM(dims, F32)

    params = pltpu.CompilerParams(vmem_limit_bytes=16 << 20)

    def call(kernel, outs, specs, name, *args, scratches=(), out_specs=None):
        return pl.pallas_call(
            kernel,
            out_shape=tuple(outs),
            in_specs=specs,
            out_specs=tuple(out_specs or [VM] * len(outs)),
            scratch_shapes=list(scratches),
            compiler_params=params,
            name=name,
        )(*args)

    def far(value):
        return pltpu.with_memory_space_constraint(value, pltpu.HBM)

    def near(value):
        return pltpu.with_memory_space_constraint(value, pltpu.VMEM)

    block_scratch = [scratch(slots, tile, tile), pltpu.SemaphoreType.DMA((slots // CHUNK,))]
    blocks = far(block_matrices[0])
    everyone = lax.all_to_all(
        jnp.broadcast_to(tile_column[None], (devices, 1, slots)), GROUP, 0, 0, tiled=True
    )
    ids, prod, sec, dual_t, bound_t, own, own_sum, usable = call(
        functools.partial(start_kernel, (tile, own2, count_first, count_second)),
        [shape(1, slots), shape(slots, tile), shape(count_second + 3 * own2, tile), shape(tile, tile),
         shape(tile, tile), shape(slots, slots), shape(slots, tile), shape(1, slots)],
        [HB, SM, SM, VM] + [HB] * 6 + [SM],
        "start",
        blocks, slot_row_block, block_count, tile_column, far(dual_start[0]), far(row_bound[0]), far(cost_second[0]),
        far(upper_second[0]), far(second_start[0]), far(intensity), carbon_scenario,
        scratches=[scratch(local_rows, tile, tile), scratch(slots, 8, tile), scratch(2, tile, tile),
                   scratch(own2, tile), block_scratch[0], pltpu.SemaphoreType.DMA((6,)), block_scratch[1]],
    )
    firsts = (cost_first, lower_first, upper_first, first_start)
    width = -(-(most * 4 + keep + 1) // 8) * 8
    send, pick = call(
        functools.partial(plan_kernel, (devices, slots, shard, most, keep, GROUP)),
        [shape(devices, width, tile), shape(keep * devices, slots)],
        [VM] * 8,
        "plan",
        everyone, ids, usable, own_sum, *firsts,
        scratches=[scratch(128, 128), scratch(devices, slots)],
    )
    answer = lax.all_to_all(send, GROUP, 0, 0, tiled=True)
    base, place, reply_pick, stack, kept, scale = call(
        functools.partial(side_kernel, (devices, slots, shard, most, GROUP)),
        [shape(shard, tile), shape(most * devices, shard), shape(most * devices, slots),
         shape(slots + keep * devices, slots), pltpu.VMEM((slots, tile, tile), jnp.int16), shape(slots, tile)],
        [VM] * 8 + [HB, SM],
        "side",
        everyone, ids, own, pick, *firsts, blocks, block_count,
        scratches=[scratch(slots, 8, tile)] + block_scratch,
    )

    def swap(value):
        return [lax.ppermute(value, PAIR, [(i, i ^ k) for i in range(pairs)]) for k in peers]

    sec_in = swap(sec)
    step_sizes = (devices, slots, count_first, count_second, own2, peers, most, keep, cells)
    step_scratch = (
        [scratch(local_rows, tile, tile), scratch(slots, 8, tile), scratch(3, count_second, tile)]
        + [scratch(local_rows, tile, tile)] * ACCS
        + [scratch(tile, tile)]
    )
    reply_width = -(-(most + 1) // 8) * 8

    def exchange(value):
        gathered = lax.all_gather(value, GROUP, axis=0, tiled=True)
        match = (everyone.astype(F32).reshape(1, -1) == ids.reshape(-1, 1)).astype(F32)
        return jnp.dot(match, gathered, precision=lax.Precision.HIGHEST)

    def run_step(step, direct, args):
        first_step, last_step = step == 0, step == ITERS - 1
        if last_step:
            outs = [shape(devices, reply_width, tile), shape(1, own2, tile), shape(1, local_rows, tile)]
        else:
            outs = [shape(slots, tile), shape(count_second, tile), shape(tile, tile), shape(1, tile),
                    shape(count_second, tile), shape(slots, tile)]
            if not direct:
                outs.append(shape(devices, keep, tile))
        specs = [VM] * len(outs)
        if first_step:
            lead = [shape(slots, tile)] * 3 + [shape(keep * devices, slots)] + [shape(count_second, tile)] * 2
            lead_specs = [VM] * 6
            if not direct:
                lead.append(jax.ShapeDtypeStruct((1, 1), jnp.int32))
                lead_specs.append(SM)
            outs, specs = lead + outs, lead_specs + specs
        return list(call(
            functools.partial(step_kernel, step_sizes, first_step, last_step, direct),
            outs,
            [VM, VM, SM] + [VM] * (len(args) - 3),
            "step",
            *args,
            scratches=step_scratch,
            out_specs=specs,
        ))

    def begin(direct, answer, own_sum, dual_t, sec, sec_in):
        args = [near(kept), scale, slot_row_block, ids, dual_t, bound_t, answer, own_sum, sec] + list(sec_in)
        if not direct:
            args.append(stack)
        return run_step(0, direct, args)

    def proceed(direct, fixed, state):
        squares = []
        for step in range(1, ITERS):
            x, y, dual_t, square, sec, own_sum = state[:6]
            squares.append(square)
            cost, lower, upper, match, cost2, upper2 = fixed
            args = [near(kept), scale, slot_row_block, ids, dual_t, bound_t, x, cost, lower, upper, match, y, cost2, upper2]
            if direct:
                args.append(exchange(own_sum))
            else:
                args += [own_sum, lax.all_to_all(state[6], GROUP, 0, 0, tiled=True)]
            args += [sec] + swap(sec)
            if step == ITERS - 1:
                args += [reply_pick] + squares
            elif not direct:
                args.append(stack)
            state = run_step(step, direct, args)
        reply, y, dual = state
        return lax.all_to_all(reply, GROUP, 0, 0, tiled=True), y, dual

    def general(operands):
        (answer, prod, dual_t, sec, sec_in), _ = operands
        results = begin(True, answer, exchange(prod), dual_t, sec, sec_in)
        return proceed(True, results[:6], results[6:])

    def usual(operands):
        _, results = operands
        return proceed(False, results[:6], results[7:])

    results = begin(False, answer, own_sum, dual_t, sec, sec_in)
    reply, y, dual = lax.cond(
        results[6][0, 0] > 0, general, usual, ((answer, prod, dual_t, sec, sec_in), results)
    )
    first_final, norms = call(
        functools.partial(finish_kernel, (devices, most, cells)),
        [shape(shard, tile), shape(ITERS)],
        [VM] * 3,
        "finish",
        reply, base, place,
        out_specs=[VM, SM],
    )
    return first_final, y, dual, norms


def solution(mesh):
    return jax.shard_map(
        shards,
        mesh=mesh,
        in_specs=(
            P(("grp", "scen"), ("blk", "sub"), None, None),
            P(("grp", "scen"), ("blk", "sub")),
            P(("grp", "scen"), ("blk", "sub")),
            P(("grp", "scen"), ("blk", "sub")),
            P(("grp", "scen")),
            P(None, ("blk", "sub"), None),
            P(("grp", "scen", "blk", "sub"), None),
            P(("grp", "scen", "blk", "sub"), None),
            P(("grp", "scen", "blk", "sub"), None),
            P(("grp", "scen"), ("blk", "sub"), None),
            P(("grp", "scen"), ("blk", "sub"), None),
            P(("grp", "scen"), ("blk", "sub"), None),
            P(("grp", "scen", "blk", "sub"), None),
            P(("grp", "scen"), ("blk", "sub"), None),
            P(("grp", "scen"), ("blk", "sub"), None),
        ),
        out_specs=(
            P(("grp", "scen", "blk", "sub"), None),
            P(("grp", "scen"), ("blk", "sub"), None),
            P(("grp", "scen"), ("blk", "sub"), None),
            P("grp"),
        ),
        check_vma=False,
    )
```

time: 84.1 us -> 74.3 us (0.88)
  local copies, waits for them, and re-layouts: 6.05 us -> 1.99 us
  waiting for transfers between devices: 15.3 us -> 13.2 us
  other arithmetic: 2.01 us -> 0 us
    unnamed x22 -> x12, local copies, waits for them, and re-layouts: 4.34 us -> 0.67 us
    all_to_all x1, waiting for transfers between devices: 6.15 us -> 3.12 us  [shards(): answer = lax.all_to_all(send, GROUP, 0, 0, tiled=True)]
  transfers between devices with their start and end apart: 13 -> 13, of which waited for: 7 -> 9; matrix products, arithmetic and copies ran while one was open for 2% -> 0% of each run, Pallas kernels for 5% -> 10%
where the time goes in v2:
time: 74.3 us; the launch traced here: 73.8 us
  starting transfers between devices  25.8 us (35%)
  Pallas kernels  19.7 us (27%)
  waiting for transfers between devices  13.2 us (18%)
  blocking collectives  10.1 us (14%)
  between operations  2.87 us (4%)
  local copies, waits for them, and re-layouts  1.99 us (3%)
    pallas_call x7, Pallas kernels, call(): pl.pallas_call(kernel, out_shape=tuple(outs), in_specs=specs, out_specs=t...  19.7 us
    all_to_all x1, blocking collectives, proceed(): return (lax.all_to_all(reply, GROUP, 0, 0, tiled=True), y, dual)  10.1 us
    all_to_all x1, starting transfers between devices, shards(): lax.all_to_all(jnp.broadcast_to(tile_column[None], (devices, 1, slots)),...  7.36 us
    all_to_all x2, starting transfers between devices, proceed(): args += [own_sum, lax.all_to_all(state[6], GROUP, 0, 0, tiled=True)]  6.96 us
    ppermute x9, waiting for transfers between devices, swap(): lax.ppermute(value, PAIR, [(i, i ^ k) for i in range(pairs)])  6.58 us
    ppermute x9, starting transfers between devices, swap(): lax.ppermute(value, PAIR, [(i, i ^ k) for i in range(pairs)])  6.17 us
    all_to_all x1, starting transfers between devices, shards(): answer = lax.all_to_all(send, GROUP, 0, 0, tiled=True)  5.33 us
    all_to_all x1, waiting for transfers between devices, shards(): answer = lax.all_to_all(send, GROUP, 0, 0, tiled=True)  3.12 us
  transfers between devices with their start and end apart: 13, of which 9 were waited for; matrix products, arithmetic and copies ran while one was open for 0% of the time, Pallas kernels for 10%

profile of v2, /device:TPU:0, one launch (start us, length us, event | category | flops | bytes accessed | tf_op | source)
XLA Modules:
  0.0 73.8 jit_solution(12131185676050067145)
XLA Ops:
  0.7 1.3 %broadcast_in_dim.9 = s32[16,1,64]{2,1,0:T(1,128)} broadcast(s32[64]{0:T(128)} %bitcast.12), dimensions={2} | broadcast | bytes 4352 | tf_op jit(solution)/shard_map/broadcast_in_dim | solution.py:451
  2.0 7.4 %all-to-all-start.4 = ((s32[16,1,64]{2,1,0:T(1,128)}), s32[16,1,64]{2,1,0:T(1,128)S(1)}, u32[]{:S(2)}, u32[]{:S(2)}) async-start(s32[16,1,64]{2,1,0:T(1,128)} %broadcast_in_dim.9), calls=%async_computation.4 | async-start | bytes 16384 | tf_op jit(solution)/shard_map/all_to_all | solution.py:450
  10.6 0.0 copy-start.4
  10.7 0.6 copy-done.4
  11.3 3.7 %start.1 = (f32[1,64]{1,0:T(1,128)S(1)}, f32[64,128]{1,0:T(8,128)S(1)}, f32[56,128]{1,0:T(8,128)S(1)}, f32[128,128]{1,0:T(8,128)S(1)}, f32[128,128]{1,0:T(8,128)...) custom-call(f32[64,128,128]{2,1,0:T(8,128)} %bitcast.13, s32[1,64]{1,0:T(1,128)} %refs_2_.1, ...), custom_call_target="tpu_custom_call" | custom-call | tf_op jit(solution)/shard_map/start/pallas_call | solution.py:432
  15.0 0.7 all-to-all-done.4.everyone
  15.7 1.7 %plan.1 = (f32[16,24,128]{2,1,0:T(8,128)}, f32[64,64]{1,0:T(8,128)S(1)}) custom-call(s32[16,1,64]{2,1,0:T(1,128)S(1)} %all-to-all-done.4.everyone, f32[1,64]{1,0:T(1,128)S(1)} %get-tuple-element.172.ids.refs_3_, f32[1,64]{1,0:T(1,128)S(1)} %get-tuple-element.174.usable, f32[64,128]{1,0:T(8,128)S(1)} %get-tuple-element.175.total.refs_7_, ...), custom_call_target="tpu_custom_call" | custom-call | tf_op jit(solution)/shard_map/plan/pallas_call | solution.py:432
  17.4 5.3 %all-to-all-start.5 = ((f32[16,24,128]{2,1,0:T(8,128)}), f32[16,24,128]{2,1,0:T(8,128)S(1)}, u32[]{:S(2)}, u32[]{:S(2)}) async-start(f32[16,24,128]{2,1,0:T(8,128)} %get-tuple-element.181), calls=%async_computation.5 | async-start | bytes 393216 | tf_op jit(solution)/shard_map/all_to_all | solution.py:474
  22.7 0.4 collective-permute-start.12
  23.1 1.7 %collective-permute-start.13 = (f32[56,128]{1,0:T(8,128)S(1)}, f32[56,128]{1,0:T(8,128)S(1)}, u32[]{:S(2)}, u32[]{:S(2)}) collective-permute-start(f32[56,128]{1,0:T(8,128)S(1)} %get-tuple-element.182.refs_8_), channel_id=1, source_target_pairs={{0,2},{1,3},{2,0},{3,1},{4,6},{5,7},{6,4},{7,5},{8,10},{9,11},{10,... | collective-permute-start | bytes 86024 | tf_op jit(solution)/shard_map/ppermute | solution.py:486
  24.8 0.0 collective-permute-start.14
  24.8 3.5 %side.1 = (f32[256,128]{1,0:T(8,128)S(1)}, f32[64,256]{1,0:T(8,128)S(1)}, f32[64,64]{1,0:T(8,128)S(1)}, f32[128,64]{1,0:T(8,128)S(1)}, s16[64,128,128]{2,1,0:T(8,128)(2,1)S(1)}, /*index=5*/f32[64,128]{1,0:T(8,128)S(1)}) custom-call(s32[16,1,64]{2,1,0:T(1,128)S(1)} %all-to-all-done.4.everyone, f32[1,64]{1,0:T(1,128)S(1)} %get-tuple-element.172.ids.refs_3_, ...), custom_call_target="tpu_custom_call" | custom-call | tf_op jit(solution)/shard_map/side/pallas_call | solution.py:432
  28.3 0.2 collective-permute-done.14.refs_11_
  28.6 3.1 %all-to-all-done.5.refs_6_ = f32[16,24,128]{2,1,0:T(8,128)S(1)} async-done(((f32[16,24,128]{2,1,0:T(8,128)}), f32[16,24,128]{2,1,0:T(8,128)S(1)}, u32[]{:S(2)}, u32[]{:S(2)}) %all-to-all-start.5) | async-done | bytes 196640 | tf_op jit(solution)/shard_map/all_to_all | solution.py:474
  31.7 3.7 %step.11 = (f32[64,128]{1,0:T(8,128)S(1)}, f32[64,128]{1,0:T(8,128)S(1)}, f32[64,128]{1,0:T(8,128)S(1)}, f32[64,64]{1,0:T(8,128)S(1)}, f32[32,128]{1,0:T(8,128)S...) custom-call(s16[64,128,128]{2,1,0:T(8,128)(2,1)S(1)} %get-tuple-elem, ...), custom_call_target="tpu_custom_call" | custom-call | tf_op jit(solution)/shard_map/step/pallas_call | solution.py:432
  36.0 36.6 %conditional.1 = (f32[16,8,128]{2,1,0:T(8,128)S(1)}, f32[1,8,128]{2,1,0:T(8,128)}, f32[1,8,128]{2,1,0:T(8,128)}) conditional(s32[]{:T(128)} %bitcast.8, (f32[16,4,128]{2,1,0:T(4,128)}, f32[32,128]{1,0:T(8,128)S(1)}, s16[64,128,128]{2,1,0:T(8,128)(2,1)S(1)}, f32[64,128]{1,0:T(8,128)S(1)}, s32[1,64]{1,0:T(1,128)S(1)}, /*index=5*/f32[1,64]{1,0:T(1,128)S(1)}, ...), branch_computations={%region_0.0_spmd, %region_1.0_spmd} | conditional | flops 302187520 | bytes 3896328 | solution.py:565
  36.0 3.5 %all-to-all-start = ((f32[16,4,128]{2,1,0:T(4,128)}), f32[16,4,128]{2,1,0:T(4,128)S(1)}, u32[]{:S(2)}, u32[]{:S(2)}) async-start(f32[16,4,128]{2,1,0:T(4,128)} %get-tuple-element.83), calls=%async_computation | async-start | bytes 65536 | tf_op jit(solution)/shard_map/cond/branch_0_fun/all_to_all | solution.py:545
  39.6 0.3 collective-permute-start
  39.9 1.7 %collective-permute-start.1 = (f32[32,128]{1,0:T(8,128)S(1)}, f32[32,128]{1,0:T(8,128)S(1)}, u32[]{:S(2)}, u32[]{:S(2)}) collective-permute-start(f32[32,128]{1,0:T(8,128)S(1)} %get-tuple-element.84.refs_16_), channel_id=1, source_target_pairs={{0,2},{1,3},{2,0},{3,1},{4,6},{5,7},{6,4},{7,5},{8,10},{9,11},{10,... | collective-permute-start | bytes 49160 | tf_op jit(solution)/shard_map/cond/branch_0_fun/ppermute | solution.py:486
  41.6 2.1 %collective-permute-done.1.refs_18_ = f32[32,128]{1,0:T(8,128)S(1)} collective-permute-done((f32[32,128]{1,0:T(8,128)S(1)}, f32[32,128]{1,0:T(8,128)S(1)}, u32[]{:S(2)}, u32[]{:S(2)}) %collective-permute-start.1) | collective-permute-done | bytes 16416 | tf_op jit(solution)/shard_map/cond/branch_0_fun/ppermute | solution.py:486
  43.6 1.1 %collective-permute-done.2.refs_19_ = f32[32,128]{1,0:T(8,128)S(1)} collective-permute-done((f32[32,128]{1,0:T(8,128)S(1)}, f32[32,128]{1,0:T(8,128)S(1)}, u32[]{:S(2)}, u32[]{:S(2)}) %collective-permute-start.2) | collective-permute-done | bytes 16416 | tf_op jit(solution)/shard_map/cond/branch_0_fun/ppermute | solution.py:486
  44.7 1.4 %all-to-all-done.refs_15_ = f32[16,4,128]{2,1,0:T(4,128)S(1)} async-done(((f32[16,4,128]{2,1,0:T(4,128)}), f32[16,4,128]{2,1,0:T(4,128)S(1)}, u32[]{:S(2)}, u32[]{:S(2)}) %all-to-all-start) | async-done | bytes 32800 | tf_op jit(solution)/shard_map/cond/branch_0_fun/all_to_all | solution.py:545
  46.2 3.4 %step.6 = (f32[64,128]{1,0:T(8,128)S(1)}, f32[32,128]{1,0:T(8,128)S(1)}, f32[128,128]{1,0:T(8,128)S(1)}, f32[1,128]{1,0:T(1,128)S(1)}, f32[32,128]{1,0:T(8,128)S...) custom-call(s16[64,128,128]{2,1,0:T(8,128)(2,1)S(1)} %get-tuple-element.68.refs_0_, ...), custom_call_target="tpu_custom_call" | custom-call | tf_op jit(solution)/shard_map/cond/branch_0_fun/step/pallas_call | solution.py:432
  49.6 3.5 %all-to-all-start.1 = ((f32[16,4,128]{2,1,0:T(4,128)}), f32[16,4,128]{2,1,0:T(4,128)S(1)}, u32[]{:S(2)}, u32[]{:S(2)}) async-start(f32[16,4,128]{2,1,0:T(4,128)} %get-tuple-element.90), calls=%async_computation.1 | async-start | bytes 65536 | tf_op jit(solution)/shard_map/cond/branch_0_fun/all_to_all | solution.py:545
  53.1 0.4 collective-permute-start.3
  53.5 1.7 %collective-permute-start.4 = (f32[32,128]{1,0:T(8,128)S(1)}, f32[32,128]{1,0:T(8,128)S(1)}, u32[]{:S(2)}, u32[]{:S(2)}) collective-permute-start(f32[32,128]{1,0:T(8,128)S(1)} %get-tuple-element.91.refs_16_), channel_id=1, source_target_pairs={{0,2},{1,3},{2,0},{3,1},{4,6},{5,7},{6,4},{7,5},{8,10},{9,11},{10,... | collective-permute-start | bytes 49160 | tf_op jit(solution)/shard_map/cond/branch_0_fun/ppermute | solution.py:486
  55.1 2.1 %collective-permute-done.4.refs_18_ = f32[32,128]{1,0:T(8,128)S(1)} collective-permute-done((f32[32,128]{1,0:T(8,128)S(1)}, f32[32,128]{1,0:T(8,128)S(1)}, u32[]{:S(2)}, u32[]{:S(2)}) %collective-permute-start.4) | collective-permute-done | bytes 16416 | tf_op jit(solution)/shard_map/cond/branch_0_fun/ppermute | solution.py:486
  57.2 1.1 %collective-permute-done.5.refs_19_ = f32[32,128]{1,0:T(8,128)S(1)} collective-permute-done((f32[32,128]{1,0:T(8,128)S(1)}, f32[32,128]{1,0:T(8,128)S(1)}, u32[]{:S(2)}, u32[]{:S(2)}) %collective-permute-start.5) | collective-permute-done | bytes 16416 | tf_op jit(solution)/shard_map/cond/branch_0_fun/ppermute | solution.py:486
  58.3 1.4 %all-to-all-done.1.refs_15_ = f32[16,4,128]{2,1,0:T(4,128)S(1)} async-done(((f32[16,4,128]{2,1,0:T(4,128)}), f32[16,4,128]{2,1,0:T(4,128)S(1)}, u32[]{:S(2)}, u32[]{:S(2)}) %all-to-all-start.1) | async-done | bytes 32800 | tf_op jit(solution)/shard_map/cond/branch_0_fun/all_to_all | solution.py:545
  59.7 2.8 %step.7 = (f32[16,8,128]{2,1,0:T(8,128)S(1)}, f32[1,8,128]{2,1,0:T(8,128)}, f32[1,8,128]{2,1,0:T(8,128)}) custom-call(s16[64,128,128]{2,1,0:T(8,128)(2,1)S(1)} %get-tuple-element.68.refs_0_, f32[64,128]{1,0:T(8,128)S(1)} %get-tuple-element.69.refs_1_, s32[1,64]{1,0:T(1,128)S(1)} %get-tuple-element.70.refs_2_, f32[1,64]{1,0:T(1,128)S(1)} %get-tuple-element.71.refs_3_, ...), custom_call_target="tpu_custom_call" | custom-call | tf_op jit(solution)/shard_map/cond/branch_0_fun/step/pallas_call | solution.py:432
  62.5 10.1 %all_to_all.26 = f32[16,8,128]{2,1,0:T(8,128)S(1)} all-to-all(f32[16,8,128]{2,1,0:T(8,128)S(1)} %get-tuple-element.95), channel_id=1, replica_groups=mesh['grp'=2,'scen'=4,'blk'=2,'sub'=2] {'scen','blk','sub'}, dimensions={0} | all-to-all | bytes 131072 | tf_op jit(solution)/shard_map/cond/branch_0_fun/all_to_all | solution.py:553
  72.6 1.0 %finish.1 = (f32[256,128]{1,0:T(8,128)}, f32[3]{0:T(128)}) custom-call(f32[16,8,128]{2,1,0:T(8,128)S(1)} %get-tuple-element.200.reply, f32[256,128]{1,0:T(8,128)S(1)} %get-tuple-element.201.base, f32[64,256]{1,0:T(8,128)S(1)} %get-tuple-element.202.place), custom_call_target="tpu_custom_call" | custom-call | tf_op jit(solution)/shard_map/finish/pallas_call | solution.py:432
  (16 shorter events, 0.0 us)
Async XLA Ops:
  0.6 15.1 %copy-start = (f32[256,128]{1,0:T(8,128)S(1)}, f32[256,128]{1,0:T(8,128)}, u32[]{:S(2)}) copy-start(f32[256,128]{1,0:T(8,128)} %cost.3) | copy-start | bytes 393220
  0.6 15.1 %copy-start.1 = (f32[256,128]{1,0:T(8,128)S(1)}, f32[256,128]{1,0:T(8,128)}, u32[]{:S(2)}) copy-start(f32[256,128]{1,0:T(8,128)} %lower.3) | copy-start | bytes 393220
  0.7 15.0 %copy-start.2 = (f32[256,128]{1,0:T(8,128)S(1)}, f32[256,128]{1,0:T(8,128)}, u32[]{:S(2)}) copy-start(f32[256,128]{1,0:T(8,128)} %upper.3) | copy-start | bytes 393220
  0.7 15.0 %copy-start.3 = (f32[256,128]{1,0:T(8,128)S(1)}, f32[256,128]{1,0:T(8,128)}, u32[]{:S(2)}) copy-start(f32[256,128]{1,0:T(8,128)} %first.3) | copy-start | bytes 393220
  2.0 13.7 %all-to-all-start.4 = ((s32[16,1,64]{2,1,0:T(1,128)}), s32[16,1,64]{2,1,0:T(1,128)S(1)}, u32[]{:S(2)}, u32[]{:S(2)}) async-start(s32[16,1,64]{2,1,0:T(1,128)} %broadcast_in_dim.9), calls=%async_computation.4 | async-start | bytes 16384 | tf_op jit(solution)/shard_map/all_to_all | solution.py:450
  10.6 0.7 copy-start.4
  11.3 20.4 %copy-start.5 = (s32[1,64]{1,0:T(1,128)S(1)}, s32[1,64]{1,0:T(1,128)}, u32[]{:S(2)}) copy-start(s32[1,64]{1,0:T(1,128)} %refs_2_.1) | copy-start | bytes 772
  17.4 14.3 %all-to-all-start.5 = ((f32[16,24,128]{2,1,0:T(8,128)}), f32[16,24,128]{2,1,0:T(8,128)S(1)}, u32[]{:S(2)}, u32[]{:S(2)}) async-start(f32[16,24,128]{2,1,0:T(8,128)} %get-tuple-element.181), calls=%async_computation.5 | async-start | bytes 393216 | tf_op jit(solution)/shard_map/all_to_all | solution.py:474
  22.7 5.6 %collective-permute-start.12 = (f32[56,128]{1,0:T(8,128)S(1)}, f32[56,128]{1,0:T(8,128)S(1)}, u32[]{:S(2)}, u32[]{:S(2)}) collective-permute-start(f32[56,128]{1,0:T(8,128)S(1)} %get-tuple-element.182.refs_8_), channel_id=1, source_target_pairs={{0,1},{1,0},{2,3},{3,2},{4,5},{5,4},{6,7},{7,6},{8,9},{9,8},{10,11... | collective-permute-start | bytes 86024 | tf_op jit(solution)/shard_map/ppermute | solution.py:486
  23.1 5.2 %collective-permute-start.13 = (f32[56,128]{1,0:T(8,128)S(1)}, f32[56,128]{1,0:T(8,128)S(1)}, u32[]{:S(2)}, u32[]{:S(2)}) collective-permute-start(f32[56,128]{1,0:T(8,128)S(1)} %get-tuple-element.182.refs_8_), channel_id=1, source_target_pairs={{0,2},{1,3},{2,0},{3,1},{4,6},{5,7},{6,4},{7,5},{8,10},{9,11},{10,... | collective-permute-start | bytes 86024 | tf_op jit(solution)/shard_map/ppermute | solution.py:486
  24.8 3.8 %collective-permute-start.14 = (f32[56,128]{1,0:T(8,128)S(1)}, f32[56,128]{1,0:T(8,128)S(1)}, u32[]{:S(2)}, u32[]{:S(2)}) collective-permute-start(f32[56,128]{1,0:T(8,128)S(1)} %get-tuple-element.182.refs_8_), channel_id=1, source_target_pairs={{0,3},{1,2},{2,1},{3,0},{4,7},{5,6},{6,5},{7,4},{8,11},{9,10},{10,... | collective-permute-start | bytes 86024 | tf_op jit(solution)/shard_map/ppermute | solution.py:486
  36.0 10.1 %all-to-all-start = ((f32[16,4,128]{2,1,0:T(4,128)}), f32[16,4,128]{2,1,0:T(4,128)S(1)}, u32[]{:S(2)}, u32[]{:S(2)}) async-start(f32[16,4,128]{2,1,0:T(4,128)} %get-tuple-element.83), calls=%async_computation | async-start | bytes 65536 | tf_op jit(solution)/shard_map/cond/branch_0_fun/all_to_all | solution.py:545
  39.6 2.0 %collective-permute-start = (f32[32,128]{1,0:T(8,128)S(1)}, f32[32,128]{1,0:T(8,128)S(1)}, u32[]{:S(2)}, u32[]{:S(2)}) collective-permute-start(f32[32,128]{1,0:T(8,128)S(1)} %get-tuple-element.84.refs_16_), channel_id=1, source_target_pairs={{0,1},{1,0},{2,3},{3,2},{4,5},{5,4},{6,7},{7,6},{8,9},{9,8},{10,11... | collective-permute-start | bytes 49160 | tf_op jit(solution)/shard_map/cond/branch_0_fun/ppermute | solution.py:486
  39.9 3.8 %collective-permute-start.1 = (f32[32,128]{1,0:T(8,128)S(1)}, f32[32,128]{1,0:T(8,128)S(1)}, u32[]{:S(2)}, u32[]{:S(2)}) collective-permute-start(f32[32,128]{1,0:T(8,128)S(1)} %get-tuple-element.84.refs_16_), channel_id=1, source_target_pairs={{0,2},{1,3},{2,0},{3,1},{4,6},{5,7},{6,4},{7,5},{8,10},{9,11},{10,... | collective-permute-start | bytes 49160 | tf_op jit(solution)/shard_map/cond/branch_0_fun/ppermute | solution.py:486
  41.5 3.2 %collective-permute-start.2 = (f32[32,128]{1,0:T(8,128)S(1)}, f32[32,128]{1,0:T(8,128)S(1)}, u32[]{:S(2)}, u32[]{:S(2)}) collective-permute-start(f32[32,128]{1,0:T(8,128)S(1)} %get-tuple-element.84.refs_16_), channel_id=1, source_target_pairs={{0,3},{1,2},{2,1},{3,0},{4,7},{5,6},{6,5},{7,4},{8,11},{9,10},{10,... | collective-permute-start | bytes 49160 | tf_op jit(solution)/shard_map/cond/branch_0_fun/ppermute | solution.py:486
  49.6 10.1 %all-to-all-start.1 = ((f32[16,4,128]{2,1,0:T(4,128)}), f32[16,4,128]{2,1,0:T(4,128)S(1)}, u32[]{:S(2)}, u32[]{:S(2)}) async-start(f32[16,4,128]{2,1,0:T(4,128)} %get-tuple-element.90), calls=%async_computation.1 | async-start | bytes 65536 | tf_op jit(solution)/shard_map/cond/branch_0_fun/all_to_all | solution.py:545
  53.1 2.1 %collective-permute-start.3 = (f32[32,128]{1,0:T(8,128)S(1)}, f32[32,128]{1,0:T(8,128)S(1)}, u32[]{:S(2)}, u32[]{:S(2)}) collective-permute-start(f32[32,128]{1,0:T(8,128)S(1)} %get-tuple-element.91.refs_16_), channel_id=1, source_target_pairs={{0,1},{1,0},{2,3},{3,2},{4,5},{5,4},{6,7},{7,6},{8,9},{9,8},{10,11... | collective-permute-start | bytes 49160 | tf_op jit(solution)/shard_map/cond/branch_0_fun/ppermute | solution.py:486
  53.5 3.8 %collective-permute-start.4 = (f32[32,128]{1,0:T(8,128)S(1)}, f32[32,128]{1,0:T(8,128)S(1)}, u32[]{:S(2)}, u32[]{:S(2)}) collective-permute-start(f32[32,128]{1,0:T(8,128)S(1)} %get-tuple-element.91.refs_16_), channel_id=1, source_target_pairs={{0,2},{1,3},{2,0},{3,1},{4,6},{5,7},{6,4},{7,5},{8,10},{9,11},{10,... | collective-permute-start | bytes 49160 | tf_op jit(solution)/shard_map/cond/branch_0_fun/ppermute | solution.py:486
  55.1 3.2 %collective-permute-start.5 = (f32[32,128]{1,0:T(8,128)S(1)}, f32[32,128]{1,0:T(8,128)S(1)}, u32[]{:S(2)}, u32[]{:S(2)}) collective-permute-start(f32[32,128]{1,0:T(8,128)S(1)} %get-tuple-element.91.refs_16_), channel_id=1, source_target_pairs={{0,3},{1,2},{2,1},{3,0},{4,7},{5,6},{6,5},{7,4},{8,11},{9,10},{10,... | collective-permute-start | bytes 49160 | tf_op jit(solution)/shard_map/cond/branch_0_fun/ppermute | solution.py:486

commit v3 on v2

--- a/solution.py
+++ b/solution.py
@@ -23,11 +23,18 @@
 
 def exact_dot(a, b, contract=(1, 0)):
     dims = (((contract[0],), (contract[1],)), ((), ()))
-    return lax.dot_general(a, b, dims, precision=lax.Precision.HIGHEST, preferred_element_type=F32)
+    high = b.astype(jnp.bfloat16)
+    rest = b - high.astype(F32)
+    middle = rest.astype(jnp.bfloat16)
+    low = (rest - middle.astype(F32)).astype(jnp.bfloat16)
+    parts = jnp.concatenate([high, middle, low], axis=1)
+    out = lax.dot_general(a.astype(jnp.bfloat16), parts, dims, preferred_element_type=F32)
+    width = b.shape[1]
+    return out[:, :width] + (out[:, width : 2 * width] + out[:, 2 * width :])
 
 
 def count_dot(a, b):
-    return jnp.dot(a, b, preferred_element_type=F32)
+    return jnp.dot(a.astype(jnp.bfloat16), b.astype(jnp.bfloat16), preferred_element_type=F32)
 
 
 def iota(shape, dim):
@@ -81,9 +88,9 @@
         spread[r] = jnp.broadcast_to(dual_t[:, r : r + 1], (tile, tile))
 
 
-def start_kernel(sizes, blocks_in, rows, used, columns, dual, bound, cost2, upper2, second, intensity, carbon,
+def start_kernel(sizes, blocks_in, rows_in, used, columns, dual, bound, cost2, upper2, second, intensity, carbon,
                  ids_out, prod_out, sec_out, dual_out, bound_out, own_out, sum_out, usable_out,
-                 spread, parts, squares, prices, blocks, sems, block_sems):
+                 spread, parts, squares, prices, rows, blocks, sems, block_sems):
     tile, own2, count_first, count_second = sizes
     slots = blocks.shape[0]
     local_rows = dual.shape[0]
@@ -97,6 +104,7 @@
             (upper2, places[1]),
             (second, places[2]),
             (intensity.at[carbon[0]], prices),
+            (rows_in, rows),
         ])
     ]
     for copy in copies:
@@ -243,7 +251,7 @@
     devices, slots, count_first, count_second, own2, peers, most, keep, cells = sizes
     refs = list(refs)
     take = lambda: refs.pop(0)
-    kept, scale, rows, ids, dual_t, bound_t = [take() for _ in range(6)]
+    kept, scale, rows_in, ids, dual_t, bound_t = [take() for _ in range(6)]
     row = ids[...]
     if first_step:
         answer = take()
@@ -276,7 +284,9 @@
         send_out = None if direct else take()
     spread, parts, second_all = take(), take(), take()
     accs = [take() for _ in range(ACCS)]
-    square = take()
+    square, rows, row_sems = take(), take(), take()
+    row_copy = pltpu.make_async_copy(rows_in, rows, row_sems.at[0])
+    row_copy.start()
 
     if first_step:
         me2 = lax.axis_index(PAIR)
@@ -329,6 +339,7 @@
     for acc in accs:
         acc[...] = jnp.zeros_like(acc)
     tile = kept.shape[1]
+    row_copy.wait()
     for n in range(slots):
         r = rows[0, n]
         acc = accs[n % ACCS]
@@ -454,12 +465,12 @@
         functools.partial(start_kernel, (tile, own2, count_first, count_second)),
         [shape(1, slots), shape(slots, tile), shape(count_second + 3 * own2, tile), shape(tile, tile),
          shape(tile, tile), shape(slots, slots), shape(slots, tile), shape(1, slots)],
-        [HB, SM, SM, VM] + [HB] * 6 + [SM],
+        [HB, HB, SM, VM] + [HB] * 6 + [SM],
         "start",
         blocks, slot_row_block, block_count, tile_column, far(dual_start[0]), far(row_bound[0]), far(cost_second[0]),
         far(upper_second[0]), far(second_start[0]), far(intensity), carbon_scenario,
         scratches=[scratch(local_rows, tile, tile), scratch(slots, 8, tile), scratch(2, tile, tile),
-                   scratch(own2, tile), block_scratch[0], pltpu.SemaphoreType.DMA((6,)), block_scratch[1]],
+                   scratch(own2, tile), pltpu.SMEM((1, slots), jnp.int32), block_scratch[0], pltpu.SemaphoreType.DMA((7,)), block_scratch[1]],
     )
     firsts = (cost_first, lower_first, upper_first, first_start)
     width = -(-(most * 4 + keep + 1) // 8) * 8
@@ -490,7 +501,7 @@
     step_scratch = (
         [scratch(local_rows, tile, tile), scratch(slots, 8, tile), scratch(3, count_second, tile)]
         + [scratch(local_rows, tile, tile)] * ACCS
-        + [scratch(tile, tile)]
+        + [scratch(tile, tile), pltpu.SMEM((1, slots), jnp.int32), pltpu.SemaphoreType.DMA((1,))]
     )
     reply_width = -(-(most + 1) // 8) * 8
 
@@ -519,7 +530,7 @@
         return list(call(
             functools.partial(step_kernel, step_sizes, first_step, last_step, direct),
             outs,
-            [VM, VM, SM] + [VM] * (len(args) - 3),
+            [VM, VM, HB] + [VM] * (len(args) - 3),
             "step",
             *args,
             scratches=step_scratch,

time: 74.3 us -> 72.6 us (0.977)
  Pallas kernels: 19.7 us -> 17.8 us
  waiting for transfers between devices: 13.2 us -> 14.4 us
  starting transfers between devices: 25.8 us -> 24.8 us
    pallas_call x7, Pallas kernels: 19.7 us -> 17.8 us  [call(): pl.pallas_call(kernel, out_shape=tuple(outs), in_specs=specs, out_specs=t...]
    all_to_all x1, waiting for transfers between devices: 0.71 us -> 1.69 us  [shards(): lax.all_to_all(jnp.broadcast_to(tile_column[None], (devices, 1, slots)),...]
    all_to_all x1, starting transfers between devices: 5.33 us -> 4.35 us  [shards(): answer = lax.all_to_all(send, GROUP, 0, 0, tiled=True)]
  transfers between devices with their start and end apart: 13 -> 13, of which waited for: 9 -> 9; matrix products, arithmetic and copies ran while one was open for 0% -> 0% of each run, Pallas kernels for 10% -> 8%
where the time goes in v3:
time: 72.6 us; the launch traced here: 72.1 us
  starting transfers between devices  24.8 us (34%)
  Pallas kernels  17.8 us (25%)
  waiting for transfers between devices  14.4 us (20%)
  blocking collectives  10.1 us (14%)
  between operations  2.87 us (4%)
  local copies, waits for them, and re-layouts  1.99 us (3%)
    pallas_call x7, Pallas kernels, call(): pl.pallas_call(kernel, out_shape=tuple(outs), in_specs=specs, out_specs=t...  17.8 us
    all_to_all x1, blocking collectives, proceed(): return (lax.all_to_all(reply, GROUP, 0, 0, tiled=True), y, dual)  10.1 us
    all_to_all x1, starting transfers between devices, shards(): lax.all_to_all(jnp.broadcast_to(tile_column[None], (devices, 1, slots)),...  7.36 us
    all_to_all x2, starting transfers between devices, proceed(): args += [own_sum, lax.all_to_all(state[6], GROUP, 0, 0, tiled=True)]  6.97 us
    ppermute x9, waiting for transfers between devices, swap(): lax.ppermute(value, PAIR, [(i, i ^ k) for i in range(pairs)])  6.81 us
    ppermute x9, starting transfers between devices, swap(): lax.ppermute(value, PAIR, [(i, i ^ k) for i in range(pairs)])  6.16 us
    all_to_all x1, starting transfers between devices, shards(): answer = lax.all_to_all(send, GROUP, 0, 0, tiled=True)  4.35 us
    all_to_all x1, waiting for transfers between devices, shards(): answer = lax.all_to_all(send, GROUP, 0, 0, tiled=True)  3.12 us
  transfers between devices with their start and end apart: 13, of which 9 were waited for; matrix products, arithmetic and copies ran while one was open for 0% of the time, Pallas kernels for 8%

profile of v3, /device:TPU:0, one launch (start us, length us, event | category | flops | bytes accessed | tf_op | source)
XLA Modules:
  0.0 72.1 jit_solution(2505673188700598613)
XLA Ops:
  0.7 1.3 %broadcast_in_dim.9 = s32[16,1,64]{2,1,0:T(1,128)} broadcast(s32[64]{0:T(128)} %bitcast.12), dimensions={2} | broadcast | bytes 4352 | tf_op jit(solution)/shard_map/broadcast_in_dim | solution.py:462
  2.0 7.4 %all-to-all-start.4 = ((s32[16,1,64]{2,1,0:T(1,128)}), s32[16,1,64]{2,1,0:T(1,128)S(1)}, u32[]{:S(2)}, u32[]{:S(2)}) async-start(s32[16,1,64]{2,1,0:T(1,128)} %broadcast_in_dim.9), calls=%async_computation.4 | async-start | bytes 16384 | tf_op jit(solution)/shard_map/all_to_all | solution.py:461
  10.6 0.0 copy-start.4
  10.7 0.6 copy-done.4
  11.3 2.7 %start.1 = (f32[1,64]{1,0:T(1,128)S(1)}, f32[64,128]{1,0:T(8,128)S(1)}, f32[56,128]{1,0:T(8,128)S(1)}, f32[128,128]{1,0:T(8,128)S(1)}, f32[128,128]{1,0:T(8,128)...) custom-call(f32[64,128,128]{2,1,0:T(8,128)} %bitcast.13, s32[1,64]{1,0:T(1,128)} %refs_2_.1, ...), custom_call_target="tpu_custom_call" | custom-call | tf_op jit(solution)/shard_map/start/pallas_call | solution.py:443
  14.0 1.7 %all-to-all-done.4.everyone = s32[16,1,64]{2,1,0:T(1,128)S(1)} async-done(((s32[16,1,64]{2,1,0:T(1,128)}), s32[16,1,64]{2,1,0:T(1,128)S(1)}, u32[]{:S(2)}, u32[]{:S(2)}) %all-to-all-start.4) | async-done | bytes 4128 | tf_op jit(solution)/shard_map/all_to_all | solution.py:461
  15.7 1.4 %plan.1 = (f32[16,24,128]{2,1,0:T(8,128)}, f32[64,64]{1,0:T(8,128)S(1)}) custom-call(s32[16,1,64]{2,1,0:T(1,128)S(1)} %all-to-all-done.4.everyone, f32[1,64]{1,0:T(1,128)S(1)} %get-tuple-element.172.ids.refs_3_, f32[1,64]{1,0:T(1,128)S(1)} %get-tuple-element.174.usable, f32[64,128]{1,0:T(8,128)S(1)} %get-tuple-element.175.total.refs_7_, ...), custom_call_target="tpu_custom_call" | custom-call | tf_op jit(solution)/shard_map/plan/pallas_call | solution.py:443
  17.1 4.4 %all-to-all-start.5 = ((f32[16,24,128]{2,1,0:T(8,128)}), f32[16,24,128]{2,1,0:T(8,128)S(1)}, u32[]{:S(2)}, u32[]{:S(2)}) async-start(f32[16,24,128]{2,1,0:T(8,128)} %get-tuple-element.181), calls=%async_computation.5 | async-start | bytes 393216 | tf_op jit(solution)/shard_map/all_to_all | solution.py:485
  21.5 0.4 collective-permute-start.12
  21.9 1.7 %collective-permute-start.13 = (f32[56,128]{1,0:T(8,128)S(1)}, f32[56,128]{1,0:T(8,128)S(1)}, u32[]{:S(2)}, u32[]{:S(2)}) collective-permute-start(f32[56,128]{1,0:T(8,128)S(1)} %get-tuple-element.182.refs_8_), channel_id=1, source_target_pairs={{0,2},{1,3},{2,0},{3,1},{4,6},{5,7},{6,4},{7,5},{8,10},{9,11},{10,... | collective-permute-start | bytes 86024 | tf_op jit(solution)/shard_map/ppermute | solution.py:497
  23.6 0.0 collective-permute-start.14
  23.6 3.3 %side.1 = (f32[256,128]{1,0:T(8,128)S(1)}, f32[64,256]{1,0:T(8,128)S(1)}, f32[64,64]{1,0:T(8,128)S(1)}, f32[128,64]{1,0:T(8,128)S(1)}, s16[64,128,128]{2,1,0:T(8,128)(2,1)S(1)}, /*index=5*/f32[64,128]{1,0:T(8,128)S(1)}) custom-call(s32[16,1,64]{2,1,0:T(1,128)S(1)} %all-to-all-done.4.everyone, f32[1,64]{1,0:T(1,128)S(1)} %get-tuple-element.172.ids.refs_3_, ...), custom_call_target="tpu_custom_call" | custom-call | tf_op jit(solution)/shard_map/side/pallas_call | solution.py:443
  26.9 0.5 collective-permute-done.14.refs_11_
  27.4 3.1 %all-to-all-done.5.refs_6_ = f32[16,24,128]{2,1,0:T(8,128)S(1)} async-done(((f32[16,24,128]{2,1,0:T(8,128)}), f32[16,24,128]{2,1,0:T(8,128)S(1)}, u32[]{:S(2)}, u32[]{:S(2)}) %all-to-all-start.5) | async-done | bytes 196640 | tf_op jit(solution)/shard_map/all_to_all | solution.py:485
  30.5 3.5 %step.11 = (f32[64,128]{1,0:T(8,128)S(1)}, f32[64,128]{1,0:T(8,128)S(1)}, f32[64,128]{1,0:T(8,128)S(1)}, f32[64,64]{1,0:T(8,128)S(1)}, f32[32,128]{1,0:T(8,128)S...) custom-call(s16[64,128,128]{2,1,0:T(8,128)(2,1)S(1)} %get-tuple-elem, ...), custom_call_target="tpu_custom_call" | custom-call | tf_op jit(solution)/shard_map/step/pallas_call | solution.py:443
  34.7 36.3 %conditional.1 = (f32[16,8,128]{2,1,0:T(8,128)S(1)}, f32[1,8,128]{2,1,0:T(8,128)}, f32[1,8,128]{2,1,0:T(8,128)}) conditional(s32[]{:T(128)} %bitcast.8, (f32[16,4,128]{2,1,0:T(4,128)}, f32[32,128]{1,0:T(8,128)S(1)}, s16[64,128,128]{2,1,0:T(8,128)(2,1)S(1)}, f32[64,128]{1,0:T(8,128)S(1)}, s32[1,64]{1,0:T(1,128)S(1)}, /*index=5*/f32[1,64]{1,0:T(1,128)S(1)}, ...), branch_computations={%region_0.0_spmd, %region_1.0_spmd} | conditional | flops 302187520 | bytes 3896328 | solution.py:576
  34.7 3.5 %all-to-all-start = ((f32[16,4,128]{2,1,0:T(4,128)}), f32[16,4,128]{2,1,0:T(4,128)S(1)}, u32[]{:S(2)}, u32[]{:S(2)}) async-start(f32[16,4,128]{2,1,0:T(4,128)} %get-tuple-element.83), calls=%async_computation | async-start | bytes 65536 | tf_op jit(solution)/shard_map/cond/branch_0_fun/all_to_all | solution.py:556
  38.2 0.3 collective-permute-start
  38.5 1.7 %collective-permute-start.1 = (f32[32,128]{1,0:T(8,128)S(1)}, f32[32,128]{1,0:T(8,128)S(1)}, u32[]{:S(2)}, u32[]{:S(2)}) collective-permute-start(f32[32,128]{1,0:T(8,128)S(1)} %get-tuple-element.84.refs_16_), channel_id=1, source_target_pairs={{0,2},{1,3},{2,0},{3,1},{4,6},{5,7},{6,4},{7,5},{8,10},{9,11},{10,... | collective-permute-start | bytes 49160 | tf_op jit(solution)/shard_map/cond/branch_0_fun/ppermute | solution.py:497
  40.2 2.1 %collective-permute-done.1.refs_18_ = f32[32,128]{1,0:T(8,128)S(1)} collective-permute-done((f32[32,128]{1,0:T(8,128)S(1)}, f32[32,128]{1,0:T(8,128)S(1)}, u32[]{:S(2)}, u32[]{:S(2)}) %collective-permute-start.1) | collective-permute-done | bytes 16416 | tf_op jit(solution)/shard_map/cond/branch_0_fun/ppermute | solution.py:497
  42.2 1.1 %collective-permute-done.2.refs_19_ = f32[32,128]{1,0:T(8,128)S(1)} collective-permute-done((f32[32,128]{1,0:T(8,128)S(1)}, f32[32,128]{1,0:T(8,128)S(1)}, u32[]{:S(2)}, u32[]{:S(2)}) %collective-permute-start.2) | collective-permute-done | bytes 16416 | tf_op jit(solution)/shard_map/cond/branch_0_fun/ppermute | solution.py:497
  43.4 1.4 %all-to-all-done.refs_15_ = f32[16,4,128]{2,1,0:T(4,128)S(1)} async-done(((f32[16,4,128]{2,1,0:T(4,128)}), f32[16,4,128]{2,1,0:T(4,128)S(1)}, u32[]{:S(2)}, u32[]{:S(2)}) %all-to-all-start) | async-done | bytes 32800 | tf_op jit(solution)/shard_map/cond/branch_0_fun/all_to_all | solution.py:556
  44.8 3.2 %step.6 = (f32[64,128]{1,0:T(8,128)S(1)}, f32[32,128]{1,0:T(8,128)S(1)}, f32[128,128]{1,0:T(8,128)S(1)}, f32[1,128]{1,0:T(1,128)S(1)}, f32[32,128]{1,0:T(8,128)S...) custom-call(s16[64,128,128]{2,1,0:T(8,128)(2,1)S(1)} %get-tuple-element.68.refs_0_, ...), custom_call_target="tpu_custom_call" | custom-call | tf_op jit(solution)/shard_map/cond/branch_0_fun/step/pallas_call | solution.py:443
  48.0 3.5 %all-to-all-start.1 = ((f32[16,4,128]{2,1,0:T(4,128)}), f32[16,4,128]{2,1,0:T(4,128)S(1)}, u32[]{:S(2)}, u32[]{:S(2)}) async-start(f32[16,4,128]{2,1,0:T(4,128)} %get-tuple-element.90), calls=%async_computation.1 | async-start | bytes 65536 | tf_op jit(solution)/shard_map/cond/branch_0_fun/all_to_all | solution.py:556
  51.5 0.4 collective-permute-start.3
  51.9 1.7 %collective-permute-start.4 = (f32[32,128]{1,0:T(8,128)S(1)}, f32[32,128]{1,0:T(8,128)S(1)}, u32[]{:S(2)}, u32[]{:S(2)}) collective-permute-start(f32[32,128]{1,0:T(8,128)S(1)} %get-tuple-element.91.refs_16_), channel_id=1, source_target_pairs={{0,2},{1,3},{2,0},{3,1},{4,6},{5,7},{6,4},{7,5},{8,10},{9,11},{10,... | collective-permute-start | bytes 49160 | tf_op jit(solution)/shard_map/cond/branch_0_fun/ppermute | solution.py:497
  53.6 2.1 %collective-permute-done.4.refs_18_ = f32[32,128]{1,0:T(8,128)S(1)} collective-permute-done((f32[32,128]{1,0:T(8,128)S(1)}, f32[32,128]{1,0:T(8,128)S(1)}, u32[]{:S(2)}, u32[]{:S(2)}) %collective-permute-start.4) | collective-permute-done | bytes 16416 | tf_op jit(solution)/shard_map/cond/branch_0_fun/ppermute | solution.py:497
  55.7 1.1 %collective-permute-done.5.refs_19_ = f32[32,128]{1,0:T(8,128)S(1)} collective-permute-done((f32[32,128]{1,0:T(8,128)S(1)}, f32[32,128]{1,0:T(8,128)S(1)}, u32[]{:S(2)}, u32[]{:S(2)}) %collective-permute-start.5) | collective-permute-done | bytes 16416 | tf_op jit(solution)/shard_map/cond/branch_0_fun/ppermute | solution.py:497
  56.7 1.4 %all-to-all-done.1.refs_15_ = f32[16,4,128]{2,1,0:T(4,128)S(1)} async-done(((f32[16,4,128]{2,1,0:T(4,128)}), f32[16,4,128]{2,1,0:T(4,128)S(1)}, u32[]{:S(2)}, u32[]{:S(2)}) %all-to-all-start.1) | async-done | bytes 32800 | tf_op jit(solution)/shard_map/cond/branch_0_fun/all_to_all | solution.py:556
  58.1 2.7 %step.7 = (f32[16,8,128]{2,1,0:T(8,128)S(1)}, f32[1,8,128]{2,1,0:T(8,128)}, f32[1,8,128]{2,1,0:T(8,128)}) custom-call(s16[64,128,128]{2,1,0:T(8,128)(2,1)S(1)} %get-tuple-element.68.refs_0_, f32[64,128]{1,0:T(8,128)S(1)} %get-tuple-element.69.refs_1_, s32[1,64]{1,0:T(1,128)S(1)} %get-tuple-element.70.refs_2_, f32[1,64]{1,0:T(1,128)S(1)} %get-tuple-element.71.refs_3_, ...), custom_call_target="tpu_custom_call" | custom-call | tf_op jit(solution)/shard_map/cond/branch_0_fun/step/pallas_call | solution.py:443
  60.9 10.1 %all_to_all.26 = f32[16,8,128]{2,1,0:T(8,128)S(1)} all-to-all(f32[16,8,128]{2,1,0:T(8,128)S(1)} %get-tuple-element.95), channel_id=1, replica_groups=mesh['grp'=2,'scen'=4,'blk'=2,'sub'=2] {'scen','blk','sub'}, dimensions={0} | all-to-all | bytes 131072 | tf_op jit(solution)/shard_map/cond/branch_0_fun/all_to_all | solution.py:564
  71.0 0.9 %finish.1 = (f32[256,128]{1,0:T(8,128)}, f32[3]{0:T(128)}) custom-call(f32[16,8,128]{2,1,0:T(8,128)S(1)} %get-tuple-element.200.reply, f32[256,128]{1,0:T(8,128)S(1)} %get-tuple-element.201.base, f32[64,256]{1,0:T(8,128)S(1)} %get-tuple-element.202.place), custom_call_target="tpu_custom_call" | custom-call | tf_op jit(solution)/shard_map/finish/pallas_call | solution.py:443
  (16 shorter events, 0.0 us)
Async XLA Ops:
  0.6 15.1 %copy-start = (f32[256,128]{1,0:T(8,128)S(1)}, f32[256,128]{1,0:T(8,128)}, u32[]{:S(2)}) copy-start(f32[256,128]{1,0:T(8,128)} %cost.3) | copy-start | bytes 393220
  0.6 15.1 %copy-start.1 = (f32[256,128]{1,0:T(8,128)S(1)}, f32[256,128]{1,0:T(8,128)}, u32[]{:S(2)}) copy-start(f32[256,128]{1,0:T(8,128)} %lower.3) | copy-start | bytes 393220
  0.7 15.0 %copy-start.2 = (f32[256,128]{1,0:T(8,128)S(1)}, f32[256,128]{1,0:T(8,128)}, u32[]{:S(2)}) copy-start(f32[256,128]{1,0:T(8,128)} %upper.3) | copy-start | bytes 393220
  0.7 15.0 %copy-start.3 = (f32[256,128]{1,0:T(8,128)S(1)}, f32[256,128]{1,0:T(8,128)}, u32[]{:S(2)}) copy-start(f32[256,128]{1,0:T(8,128)} %first.3) | copy-start | bytes 393220
  2.0 13.7 %all-to-all-start.4 = ((s32[16,1,64]{2,1,0:T(1,128)}), s32[16,1,64]{2,1,0:T(1,128)S(1)}, u32[]{:S(2)}, u32[]{:S(2)}) async-start(s32[16,1,64]{2,1,0:T(1,128)} %broadcast_in_dim.9), calls=%async_computation.4 | async-start | bytes 16384 | tf_op jit(solution)/shard_map/all_to_all | solution.py:461
  10.6 0.7 copy-start.4
  11.3 19.2 %copy-start.5 = (s32[1,64]{1,0:T(1,128)S(1)}, s32[1,64]{1,0:T(1,128)}, u32[]{:S(2)}) copy-start(s32[1,64]{1,0:T(1,128)} %refs_2_.1) | copy-start | bytes 772
  17.1 13.4 %all-to-all-start.5 = ((f32[16,24,128]{2,1,0:T(8,128)}), f32[16,24,128]{2,1,0:T(8,128)S(1)}, u32[]{:S(2)}, u32[]{:S(2)}) async-start(f32[16,24,128]{2,1,0:T(8,128)} %get-tuple-element.181), calls=%async_computation.5 | async-start | bytes 393216 | tf_op jit(solution)/shard_map/all_to_all | solution.py:485
  21.5 5.4 %collective-permute-start.12 = (f32[56,128]{1,0:T(8,128)S(1)}, f32[56,128]{1,0:T(8,128)S(1)}, u32[]{:S(2)}, u32[]{:S(2)}) collective-permute-start(f32[56,128]{1,0:T(8,128)S(1)} %get-tuple-element.182.refs_8_), channel_id=1, source_target_pairs={{0,1},{1,0},{2,3},{3,2},{4,5},{5,4},{6,7},{7,6},{8,9},{9,8},{10,11... | collective-permute-start | bytes 86024 | tf_op jit(solution)/shard_map/ppermute | solution.py:497
  21.9 5.0 %collective-permute-start.13 = (f32[56,128]{1,0:T(8,128)S(1)}, f32[56,128]{1,0:T(8,128)S(1)}, u32[]{:S(2)}, u32[]{:S(2)}) collective-permute-start(f32[56,128]{1,0:T(8,128)S(1)} %get-tuple-element.182.refs_8_), channel_id=1, source_target_pairs={{0,2},{1,3},{2,0},{3,1},{4,6},{5,7},{6,4},{7,5},{8,10},{9,11},{10,... | collective-permute-start | bytes 86024 | tf_op jit(solution)/shard_map/ppermute | solution.py:497
  23.6 3.8 %collective-permute-start.14 = (f32[56,128]{1,0:T(8,128)S(1)}, f32[56,128]{1,0:T(8,128)S(1)}, u32[]{:S(2)}, u32[]{:S(2)}) collective-permute-start(f32[56,128]{1,0:T(8,128)S(1)} %get-tuple-element.182.refs_8_), channel_id=1, source_target_pairs={{0,3},{1,2},{2,1},{3,0},{4,7},{5,6},{6,5},{7,4},{8,11},{9,10},{10,... | collective-permute-start | bytes 86024 | tf_op jit(solution)/shard_map/ppermute | solution.py:497
  34.7 10.1 %all-to-all-start = ((f32[16,4,128]{2,1,0:T(4,128)}), f32[16,4,128]{2,1,0:T(4,128)S(1)}, u32[]{:S(2)}, u32[]{:S(2)}) async-start(f32[16,4,128]{2,1,0:T(4,128)} %get-tuple-element.83), calls=%async_computation | async-start | bytes 65536 | tf_op jit(solution)/shard_map/cond/branch_0_fun/all_to_all | solution.py:556
  38.2 2.0 %collective-permute-start = (f32[32,128]{1,0:T(8,128)S(1)}, f32[32,128]{1,0:T(8,128)S(1)}, u32[]{:S(2)}, u32[]{:S(2)}) collective-permute-start(f32[32,128]{1,0:T(8,128)S(1)} %get-tuple-element.84.refs_16_), channel_id=1, source_target_pairs={{0,1},{1,0},{2,3},{3,2},{4,5},{5,4},{6,7},{7,6},{8,9},{9,8},{10,11... | collective-permute-start | bytes 49160 | tf_op jit(solution)/shard_map/cond/branch_0_fun/ppermute | solution.py:497
  38.5 3.8 %collective-permute-start.1 = (f32[32,128]{1,0:T(8,128)S(1)}, f32[32,128]{1,0:T(8,128)S(1)}, u32[]{:S(2)}, u32[]{:S(2)}) collective-permute-start(f32[32,128]{1,0:T(8,128)S(1)} %get-tuple-element.84.refs_16_), channel_id=1, source_target_pairs={{0,2},{1,3},{2,0},{3,1},{4,6},{5,7},{6,4},{7,5},{8,10},{9,11},{10,... | collective-permute-start | bytes 49160 | tf_op jit(solution)/shard_map/cond/branch_0_fun/ppermute | solution.py:497
  40.2 3.2 %collective-permute-start.2 = (f32[32,128]{1,0:T(8,128)S(1)}, f32[32,128]{1,0:T(8,128)S(1)}, u32[]{:S(2)}, u32[]{:S(2)}) collective-permute-start(f32[32,128]{1,0:T(8,128)S(1)} %get-tuple-element.84.refs_16_), channel_id=1, source_target_pairs={{0,3},{1,2},{2,1},{3,0},{4,7},{5,6},{6,5},{7,4},{8,11},{9,10},{10,... | collective-permute-start | bytes 49160 | tf_op jit(solution)/shard_map/cond/branch_0_fun/ppermute | solution.py:497
  48.0 10.1 %all-to-all-start.1 = ((f32[16,4,128]{2,1,0:T(4,128)}), f32[16,4,128]{2,1,0:T(4,128)S(1)}, u32[]{:S(2)}, u32[]{:S(2)}) async-start(f32[16,4,128]{2,1,0:T(4,128)} %get-tuple-element.90), calls=%async_computation.1 | async-start | bytes 65536 | tf_op jit(solution)/shard_map/cond/branch_0_fun/all_to_all | solution.py:556
  51.5 2.1 %collective-permute-start.3 = (f32[32,128]{1,0:T(8,128)S(1)}, f32[32,128]{1,0:T(8,128)S(1)}, u32[]{:S(2)}, u32[]{:S(2)}) collective-permute-start(f32[32,128]{1,0:T(8,128)S(1)} %get-tuple-element.91.refs_16_), channel_id=1, source_target_pairs={{0,1},{1,0},{2,3},{3,2},{4,5},{5,4},{6,7},{7,6},{8,9},{9,8},{10,11... | collective-permute-start | bytes 49160 | tf_op jit(solution)/shard_map/cond/branch_0_fun/ppermute | solution.py:497
  51.9 3.8 %collective-permute-start.4 = (f32[32,128]{1,0:T(8,128)S(1)}, f32[32,128]{1,0:T(8,128)S(1)}, u32[]{:S(2)}, u32[]{:S(2)}) collective-permute-start(f32[32,128]{1,0:T(8,128)S(1)} %get-tuple-element.91.refs_16_), channel_id=1, source_target_pairs={{0,2},{1,3},{2,0},{3,1},{4,6},{5,7},{6,4},{7,5},{8,10},{9,11},{10,... | collective-permute-start | bytes 49160 | tf_op jit(solution)/shard_map/cond/branch_0_fun/ppermute | solution.py:497
  53.6 3.2 %collective-permute-start.5 = (f32[32,128]{1,0:T(8,128)S(1)}, f32[32,128]{1,0:T(8,128)S(1)}, u32[]{:S(2)}, u32[]{:S(2)}) collective-permute-start(f32[32,128]{1,0:T(8,128)S(1)} %get-tuple-element.91.refs_16_), channel_id=1, source_target_pairs={{0,3},{1,2},{2,1},{3,0},{4,7},{5,6},{6,5},{7,4},{8,11},{9,10},{10,... | collective-permute-start | bytes 49160 | tf_op jit(solution)/shard_map/cond/branch_0_fun/ppermute | solution.py:497

commit v4 on v3

--- a/solution.py
+++ b/solution.py
@@ -17,7 +17,7 @@
 VM = pl.BlockSpec(memory_space=pltpu.VMEM)
 SM = pl.BlockSpec(memory_space=pltpu.SMEM)
 HB = pl.BlockSpec(memory_space=pl.ANY)
-ACCS = 2
+ACCS = 1
 CHUNK = 16
 
 
@@ -247,6 +247,36 @@
             kept_out[n, part, :] = level.astype(jnp.int32).astype(jnp.int16)
 
 
+def ahead_kernel(sizes, first_step, *refs):
+    count_first, count_second, own2, peers = sizes
+    refs = list(refs)
+    take = lambda: refs.pop(0)
+    ids, sec_own = take(), take()
+    sec_in = [take() for _ in peers]
+    if not first_step:
+        y_in, cost2_in, upper2_in = take(), take(), take()
+    if first_step:
+        cost2_out, upper2_out = take(), take()
+    y_out, bars_out, second_all = take(), take(), take()
+    if first_step:
+        me2 = lax.axis_index(PAIR)
+        for k, source in [(0, sec_own)] + list(zip(peers, sec_in)):
+            place = pl.multiple_of(lax.bitwise_xor(me2, k) * own2, own2)
+            for a in range(3):
+                second_all[a, pl.ds(place, own2), :] = source[pl.ds(count_second + a * own2, own2), :]
+        cost2, upper2, y = second_all[0], second_all[1], second_all[2]
+        cost2_out[...] = cost2
+        upper2_out[...] = upper2
+    else:
+        y, cost2, upper2 = y_in[...], cost2_in[...], upper2_in[...]
+    grad2 = sec_own[pl.ds(0, count_second), :]
+    for source in sec_in:
+        grad2 = grad2 + source[pl.ds(0, count_second), :]
+    y_next = jnp.clip(y - STEP_PRIMAL * (cost2 - grad2), 0.0, upper2)
+    y_out[...] = y_next
+    bars_out[...] = exact_dot(second_onehot(ids[...], count_first, count_second), 2.0 * y_next - y, (0, 0))
+
+
 def step_kernel(sizes, first_step, last_step, direct, *refs):
     devices, slots, count_first, count_second, own2, peers, most, keep, cells = sizes
     refs = list(refs)
@@ -257,17 +287,13 @@
         answer = take()
         own_sum = None if direct else take()
         gradient = take() if direct else None
-        sec_own = take()
-        sec_in = [take() for _ in range(len(peers))]
     else:
         x_in, cost_in, lower_in, upper_in, match_in = take(), take(), take(), take(), take()
-        y_in, cost2_in, upper2_in = take(), take(), take()
         if direct:
             gradient = take()
         else:
             own_sum, received = take(), take()
-        sec_own = take()
-        sec_in = [take() for _ in range(len(peers))]
+    second_bars = take()
     if not last_step:
         if not direct:
             stack_in = take()
@@ -275,36 +301,29 @@
         reply_in = take()
         squares_in = [take() for _ in range(ITERS - 1)]
     if first_step:
-        cost_out, lower_out, upper_out, match_out, cost2_out, upper2_out = [take() for _ in range(6)]
+        cost_out, lower_out, upper_out, match_out = [take() for _ in range(4)]
         flag_out = None if direct else take()
     if last_step:
-        reply_out, y_out, dual_out = take(), take(), take()
+        reply_out, dual_out = take(), take()
     else:
-        x_out, y_out, dual_out, square_out, sec_out, sum_out = [take() for _ in range(6)]
+        x_out, dual_out, square_out, sec_out, sum_out = [take() for _ in range(5)]
         send_out = None if direct else take()
-    spread, parts, second_all = take(), take(), take()
+    spread, parts = take(), take()
     accs = [take() for _ in range(ACCS)]
     square, rows, row_sems = take(), take(), take()
     row_copy = pltpu.make_async_copy(rows_in, rows, row_sems.at[0])
     row_copy.start()
 
     if first_step:
-        me2 = lax.axis_index(PAIR)
-        for k, source in [(0, sec_own)] + list(zip(peers, sec_in)):
-            place = pl.multiple_of(lax.bitwise_xor(me2, k) * own2, own2)
-            for a in range(3):
-                second_all[a, pl.ds(place, own2), :] = source[pl.ds(count_second + a * own2, own2), :]
-        cost2, upper2, y = second_all[0], second_all[1], second_all[2]
-        cost2_out[...] = cost2
-        upper2_out[...] = upper2
         id_row = answer[:, most * 4 + keep, :]
         names = jnp.concatenate([id_row[:, q : q + 1] for q in range(most)], axis=0)
         place = as_float(names == iota((most * devices, slots), 1))
-        got = []
-        for a in range(4):
-            stacked = jnp.concatenate([answer[:, q * 4 + a, :] for q in range(most)], axis=0)
-            got.append(exact_dot(place, stacked, (0, 0)))
-        cost, lower, upper, x = got
+        stacked = jnp.concatenate(
+            [jnp.concatenate([answer[:, q * 4 + a, :] for q in range(most)], axis=0) for a in range(4)], axis=1
+        )
+        got = exact_dot(place, stacked, (0, 0))
+        width = got.shape[1] // 4
+        cost, lower, upper, x = [got[:, a * width : (a + 1) * width] for a in range(4)]
         cost_out[...] = cost
         lower_out[...] = lower
         upper_out[...] = upper
@@ -316,26 +335,15 @@
             fresh = jnp.concatenate([answer[:, most * 4 + p, :] for p in range(keep)], axis=0)
     else:
         x, cost, lower, upper, match = x_in[...], cost_in[...], lower_in[...], upper_in[...], match_in[...]
-        y, cost2, upper2 = y_in[...], cost2_in[...], upper2_in[...]
         if not direct:
             fresh = jnp.concatenate([received[:, p, :] for p in range(keep)], axis=0)
     if direct:
         grad = gradient[...]
     else:
         grad = own_sum[...] + exact_dot(match, fresh, (0, 0))
-    grad2 = sec_own[pl.ds(0, count_second), :]
-    for source in sec_in:
-        grad2 = grad2 + source[pl.ds(0, count_second), :]
     x_next = jnp.clip(x - STEP_PRIMAL * (cost - grad), lower, upper)
-    y_next = jnp.clip(y - STEP_PRIMAL * (cost2 - grad2), 0.0, upper2)
     onehot = second_onehot(row, count_first, count_second)
-    bars = ((2.0 * x_next - x) + exact_dot(onehot, 2.0 * y_next - y, (0, 0))) * scale[...]
-    if last_step:
-        parts_y = second_all.at[0]
-        parts_y[...] = y_next
-        y_out[0] = parts_y[pl.ds(pl.multiple_of(lax.axis_index(PAIR) * own2, own2), own2), :]
-    else:
-        y_out[...] = y_next
+    bars = ((2.0 * x_next - x) + second_bars[...]) * scale[...]
     for acc in accs:
         acc[...] = jnp.zeros_like(acc)
     tile = kept.shape[1]
@@ -366,7 +374,7 @@
     squares = jnp.broadcast_to(jnp.sum(squares, axis=0, keepdims=True), (1, tile))
     if last_step:
         square[...] = jnp.transpose(next_dual)
-        dual_out[0] = square[pl.ds(0, local_rows), :]
+        dual_out[...] = square[pl.ds(0, local_rows), :]
         lanes = lax.broadcasted_iota(jnp.int32, (1, tile), 1)
         note = jnp.zeros((1, tile), F32)
         for k, value in enumerate([s[...] for s in squares_in] + [squares]):
@@ -391,8 +399,10 @@
             sec_out[...] = out[slots + keep * devices :]
 
 
-def finish_kernel(sizes, reply, base, place, first_out, norm_out):
-    devices, most, cells = sizes
+def finish_kernel(sizes, reply, base, place, y, dual, first_out, second_out, dual_out, norm_out):
+    devices, most, cells, own2 = sizes
+    second_out[0] = y[pl.ds(pl.multiple_of(lax.axis_index(PAIR) * own2, own2), own2), :]
+    dual_out[0] = dual[...]
     rows = jnp.concatenate([reply[:, q, :] for q in range(most)], axis=0)
     first_out[...] = base[...] + exact_dot(place[...], rows, (0, 0))
     norms = jnp.sqrt(jnp.sum(reply[:, most, :], axis=0, keepdims=True) / float(cells))
@@ -499,7 +509,7 @@
     sec_in = swap(sec)
     step_sizes = (devices, slots, count_first, count_second, own2, peers, most, keep, cells)
     step_scratch = (
-        [scratch(local_rows, tile, tile), scratch(slots, 8, tile), scratch(3, count_second, tile)]
+        [scratch(local_rows, tile, tile), scratch(slots, 8, tile)]
         + [scratch(local_rows, tile, tile)] * ACCS
         + [scratch(tile, tile), pltpu.SMEM((1, slots), jnp.int32), pltpu.SemaphoreType.DMA((1,))]
     )
@@ -513,16 +523,16 @@
     def run_step(step, direct, args):
         first_step, last_step = step == 0, step == ITERS - 1
         if last_step:
-            outs = [shape(devices, reply_width, tile), shape(1, own2, tile), shape(1, local_rows, tile)]
+            outs = [shape(devices, reply_width, tile), shape(local_rows, tile)]
         else:
-            outs = [shape(slots, tile), shape(count_second, tile), shape(tile, tile), shape(1, tile),
+            outs = [shape(slots, tile), shape(tile, tile), shape(1, tile),
                     shape(count_second, tile), shape(slots, tile)]
             if not direct:
                 outs.append(shape(devices, keep, tile))
         specs = [VM] * len(outs)
         if first_step:
-            lead = [shape(slots, tile)] * 3 + [shape(keep * devices, slots)] + [shape(count_second, tile)] * 2
-            lead_specs = [VM] * 6
+            lead = [shape(slots, tile)] * 3 + [shape(keep * devices, slots)]
+            lead_specs = [VM] * 4
             if not direct:
                 lead.append(jax.ShapeDtypeStruct((1, 1), jnp.int32))
                 lead_specs.append(SM)
@@ -537,54 +547,74 @@
             out_specs=specs,
         ))
 
-    def begin(direct, answer, own_sum, dual_t, sec, sec_in):
-        args = [near(kept), scale, slot_row_block, ids, dual_t, bound_t, answer, own_sum, sec] + list(sec_in)
+    def ahead(step, args):
+        first_step = step == 0
+        whole = shape(count_second, tile)
+        outs = [whole, whole] if first_step else []
+        outs += [whole, shape(slots, tile)]
+        return call(
+            functools.partial(ahead_kernel, (count_first, count_second, own2, peers), first_step),
+            outs,
+            [VM] * len(args),
+            "ahead",
+            *args,
+            scratches=[scratch(3, count_second, tile)],
+        )
+
+    def begin(direct, answer, own_sum, dual_t, second_bars):
+        args = [near(kept), scale, slot_row_block, ids, dual_t, bound_t, answer, own_sum, second_bars]
         if not direct:
             args.append(stack)
         return run_step(0, direct, args)
 
-    def proceed(direct, fixed, state):
+    def proceed(direct, fixed, state, second):
         squares = []
+        cost, lower, upper, match = fixed
+        cost2, upper2, y = second
         for step in range(1, ITERS):
-            x, y, dual_t, square, sec, own_sum = state[:6]
+            x, dual_t, square, sec, own_sum = state[:5]
             squares.append(square)
-            cost, lower, upper, match, cost2, upper2 = fixed
-            args = [near(kept), scale, slot_row_block, ids, dual_t, bound_t, x, cost, lower, upper, match, y, cost2, upper2]
+            y, second_bars = ahead(step, [ids, sec] + swap(sec) + [y, cost2, upper2])
+            args = [near(kept), scale, slot_row_block, ids, dual_t, bound_t, x, cost, lower, upper, match]
             if direct:
                 args.append(exchange(own_sum))
             else:
-                args += [own_sum, lax.all_to_all(state[6], GROUP, 0, 0, tiled=True)]
-            args += [sec] + swap(sec)
+                args += [own_sum, lax.all_to_all(state[5], GROUP, 0, 0, tiled=True)]
+            args.append(second_bars)
             if step == ITERS - 1:
                 args += [reply_pick] + squares
             elif not direct:
                 args.append(stack)
             state = run_step(step, direct, args)
-        reply, y, dual = state
+        reply, dual = state
         return lax.all_to_all(reply, GROUP, 0, 0, tiled=True), y, dual
 
+    cost2, upper2, y, second_bars = ahead(0, [ids, sec] + sec_in)
+
     def general(operands):
-        (answer, prod, dual_t, sec, sec_in), _ = operands
-        results = begin(True, answer, exchange(prod), dual_t, sec, sec_in)
-        return proceed(True, results[:6], results[6:])
+        (answer, prod, dual_t, second_bars), second, _ = operands
+        results = begin(True, answer, exchange(prod), dual_t, second_bars)
+        return proceed(True, results[:4], results[4:], second)
 
     def usual(operands):
-        _, results = operands
-        return proceed(False, results[:6], results[7:])
-
-    results = begin(False, answer, own_sum, dual_t, sec, sec_in)
+        _, second, results = operands
+        return proceed(False, results[:4], results[5:], second)
+
+    results = begin(False, answer, own_sum, dual_t, second_bars)
     reply, y, dual = lax.cond(
-        results[6][0, 0] > 0, general, usual, ((answer, prod, dual_t, sec, sec_in), results)
-    )
-    first_final, norms = call(
-        functools.partial(finish_kernel, (devices, most, cells)),
-        [shape(shard, tile), shape(ITERS)],
-        [VM] * 3,
+        results[4][0, 0] > 0,
+        general,
+        usual,
+        ((answer, prod, dual_t, second_bars), (cost2, upper2, y), results),
+    )
+    return call(
+        functools.partial(finish_kernel, (devices, most, cells, own2)),
+        [shape(shard, tile), shape(1, own2, tile), shape(1, local_rows, tile), shape(ITERS)],
+        [VM] * 5,
         "finish",
-        reply, base, place,
-        out_specs=[VM, SM],
-    )
-    return first_final, y, dual, norms
+        reply, base, place, y, dual,
+        out_specs=[VM, VM, VM, SM],
+    )
 
 
 def solution(mesh):

time: 72.6 us -> 71.7 us (0.988)
  waiting for transfers between devices: 14.4 us -> 13.5 us
  Pallas kernels: 17.8 us -> 17 us
    pallas_call x7 -> x10, Pallas kernels: 17.8 us -> 17 us  [call(): pl.pallas_call(kernel, out_shape=tuple(outs), in_specs=specs, out_specs=t...]
  transfers between devices with their start and end apart: 13 -> 13, of which waited for: 9 -> 9; matrix products, arithmetic and copies ran while one was open for 0% -> 0% of each run, Pallas kernels for 8% -> 10%
where the time goes in v4:
time: 71.7 us; the launch traced here: 71.2 us
  starting transfers between devices  25.4 us (35%)
  Pallas kernels  17 us (24%)
  waiting for transfers between devices  13.5 us (19%)
  blocking collectives  10.4 us (15%)
  between operations  2.88 us (4%)
  local copies, waits for them, and re-layouts  1.97 us (3%)
    pallas_call x10, Pallas kernels, call(): pl.pallas_call(kernel, out_shape=tuple(outs), in_specs=specs, out_specs=t...  17 us
    all_to_all x1, blocking collectives, proceed(): return (lax.all_to_all(reply, GROUP, 0, 0, tiled=True), y, dual)  10.4 us
    all_to_all x1, starting transfers between devices, shards(): lax.all_to_all(jnp.broadcast_to(tile_column[None], (devices, 1, slots)),...  7.36 us
    all_to_all x2, starting transfers between devices, proceed(): args += [own_sum, lax.all_to_all(state[5], GROUP, 0, 0, tiled=True)]  7.15 us
    ppermute x9, waiting for transfers between devices, swap(): lax.ppermute(value, PAIR, [(i, i ^ k) for i in range(pairs)])  6.81 us
    ppermute x9, starting transfers between devices, swap(): lax.ppermute(value, PAIR, [(i, i ^ k) for i in range(pairs)])  6.18 us
    all_to_all x1, starting transfers between devices, shards(): answer = lax.all_to_all(send, GROUP, 0, 0, tiled=True)  4.73 us
    all_to_all x1, waiting for transfers between devices, shards(): answer = lax.all_to_all(send, GROUP, 0, 0, tiled=True)  2.92 us
  transfers between devices with their start and end apart: 13, of which 9 were waited for; matrix products, arithmetic and copies ran while one was open for 0% of the time, Pallas kernels for 10%

profile of v4, /device:TPU:0, one launch (start us, length us, event | category | flops | bytes accessed | tf_op | source)
XLA Modules:
  0.0 71.2 jit_solution(13666570503127188776)
XLA Ops:
  0.7 1.3 %broadcast_in_dim.9 = s32[16,1,64]{2,1,0:T(1,128)} broadcast(s32[64]{0:T(128)} %bitcast.12), dimensions={2} | broadcast | bytes 4352 | tf_op jit(solution)/shard_map/broadcast_in_dim | solution.py:472
  2.0 7.4 %all-to-all-start.4 = ((s32[16,1,64]{2,1,0:T(1,128)}), s32[16,1,64]{2,1,0:T(1,128)S(1)}, u32[]{:S(2)}, u32[]{:S(2)}) async-start(s32[16,1,64]{2,1,0:T(1,128)} %broadcast_in_dim.9), calls=%async_computation.4 | async-start | bytes 16384 | tf_op jit(solution)/shard_map/all_to_all | solution.py:471
  10.6 0.6 copy-done.4
  11.3 3.1 %start.1 = (f32[1,64]{1,0:T(1,128)S(1)}, f32[64,128]{1,0:T(8,128)}, f32[56,128]{1,0:T(8,128)S(1)}, f32[128,128]{1,0:T(8,128)S(1)}, f32[128,128]{1,0:T(8,128)S(1)...) custom-call(f32[64,128,128]{2,1,0:T(8,128)} %bitcast.13, s32[1,64]{1,0:T(1,128)} %refs_2_.1, ...), custom_call_target="tpu_custom_call" | custom-call | tf_op jit(solution)/shard_map/start/pallas_call | solution.py:453
  14.4 1.3 %all-to-all-done.4.everyone = s32[16,1,64]{2,1,0:T(1,128)S(1)} async-done(((s32[16,1,64]{2,1,0:T(1,128)}), s32[16,1,64]{2,1,0:T(1,128)S(1)}, u32[]{:S(2)}, u32[]{:S(2)}) %all-to-all-start.4) | async-done | bytes 4128 | tf_op jit(solution)/shard_map/all_to_all | solution.py:471
  15.8 1.4 %plan.1 = (f32[16,24,128]{2,1,0:T(8,128)}, f32[64,64]{1,0:T(8,128)S(1)}) custom-call(s32[16,1,64]{2,1,0:T(1,128)S(1)} %all-to-all-done.4.everyone, f32[1,64]{1,0:T(1,128)S(1)} %get-tuple-element.172.ids.refs_0_.refs_3_, f32[1,64]{1,0:T(1,128)S(1)} %get-tuple-element.174.usable, f32[64,128]{1,0:T(8,128)S(1)} %get-tuple-element.175.total.refs_7_, ...), custom_call_target="tpu_custom_call" | custom-call | tf_op jit(solution)/shard_map/plan/pallas_call | solution.py:453
  17.2 4.7 %all-to-all-start.5 = ((f32[16,24,128]{2,1,0:T(8,128)}), f32[16,24,128]{2,1,0:T(8,128)S(1)}, u32[]{:S(2)}, u32[]{:S(2)}) async-start(f32[16,24,128]{2,1,0:T(8,128)} %get-tuple-element.181), calls=%async_computation.5 | async-start | bytes 393216 | tf_op jit(solution)/shard_map/all_to_all | solution.py:495
  21.9 0.4 collective-permute-start.12
  22.4 1.7 %collective-permute-start.13 = (f32[56,128]{1,0:T(8,128)S(1)}, f32[56,128]{1,0:T(8,128)S(1)}, u32[]{:S(2)}, u32[]{:S(2)}) collective-permute-start(f32[56,128]{1,0:T(8,128)S(1)} %get-tuple-element.182.refs_1_), channel_id=1, source_target_pairs={{0,2},{1,3},{2,0},{3,1},{4,6},{5,7},{6,4},{7,5},{8,10},{9,11},{10,... | collective-permute-start | bytes 86024 | tf_op jit(solution)/shard_map/ppermute | solution.py:507
  24.0 3.3 %side.1 = (f32[256,128]{1,0:T(8,128)S(1)}, f32[64,256]{1,0:T(8,128)S(1)}, f32[64,64]{1,0:T(8,128)S(1)}, f32[128,64]{1,0:T(8,128)S(1)}, s16[64,128,128]{2,1,0:T(8,128)(2,1)S(1)}, /*index=5*/f32[64,128]{1,0:T(8,128)S(1)}) custom-call(s32[16,1,64]{2,1,0:T(1,128)S(1)} %all-to-all-done.4.everyone, f32[1,64]{1,0:T(1,128)S(1)} %get-tuple-element.172.ids.refs_0_.refs_3_, ...), custom_call_target="tpu_custom_call" | custom-call | tf_op jit(solution)/shard_map/side/pallas_call | solution.py:453
  27.3 0.5 collective-permute-done.14.refs_4_
  27.8 0.2 ahead.9
  28.0 2.9 %all-to-all-done.5.refs_6_ = f32[16,24,128]{2,1,0:T(8,128)S(1)} async-done(((f32[16,24,128]{2,1,0:T(8,128)}), f32[16,24,128]{2,1,0:T(8,128)S(1)}, u32[]{:S(2)}, u32[]{:S(2)}) %all-to-all-start.5) | async-done | bytes 196640 | tf_op jit(solution)/shard_map/all_to_all | solution.py:495
  30.9 2.9 %step.11 = (f32[64,128]{1,0:T(8,128)S(1)}, f32[64,128]{1,0:T(8,128)S(1)}, f32[64,128]{1,0:T(8,128)S(1)}, f32[64,64]{1,0:T(8,128)S(1)}, s32[1,1]{1,0:T(1,128)}, /...) custom-call(s16[64,128,128]{2,1,0:T(8,128)(2,1)S(1)} %get-tuple-elem, ...), custom_call_target="tpu_custom_call" | custom-call | tf_op jit(solution)/shard_map/step/pallas_call | solution.py:453
  34.5 35.6 %conditional.1 = (f32[16,8,128]{2,1,0:T(8,128)S(1)}, f32[32,128]{1,0:T(8,128)S(1)}, f32[8,128]{1,0:T(8,128)S(1)}) conditional(s32[]{:T(128)} %bitcast.8, (f32[16,4,128]{2,1,0:T(4,128)}, f32[32,128]{1,0:T(8,128)S(1)}, f32[1,64]{1,0:T(1,128)S(1)}, f32[32,128]{1,0:T(8,128)S(1)}, f32[32,128]{1,0:T(8,128)S(1)}, /*index=5*/f32[32,128]{1,0:T(8,128)S(1)}, ...), branch_computations={%region_0.0_spmd, %region_1.0_spmd} | conditional | flops 302187520 | bytes 4027456 | solution.py:604
  34.5 3.5 %all-to-all-start = ((f32[16,4,128]{2,1,0:T(4,128)}), f32[16,4,128]{2,1,0:T(4,128)S(1)}, u32[]{:S(2)}, u32[]{:S(2)}) async-start(f32[16,4,128]{2,1,0:T(4,128)} %get-tuple-element.80), calls=%async_computation | async-start | bytes 65536 | tf_op jit(solution)/shard_map/cond/branch_0_fun/all_to_all | solution.py:582
  38.0 0.3 collective-permute-start
  38.3 1.7 %collective-permute-start.1 = (f32[32,128]{1,0:T(8,128)S(1)}, f32[32,128]{1,0:T(8,128)S(1)}, u32[]{:S(2)}, u32[]{:S(2)}) collective-permute-start(f32[32,128]{1,0:T(8,128)S(1)} %get-tuple-element.81.refs_1_), channel_id=1, source_target_pairs={{0,2},{1,3},{2,0},{3,1},{4,6},{5,7},{6,4},{7,5},{8,10},{9,11},{10,... | collective-permute-start | bytes 49160 | tf_op jit(solution)/shard_map/cond/branch_0_fun/ppermute | solution.py:507
  40.0 2.1 %collective-permute-done.1.refs_3_ = f32[32,128]{1,0:T(8,128)S(1)} collective-permute-done((f32[32,128]{1,0:T(8,128)S(1)}, f32[32,128]{1,0:T(8,128)S(1)}, u32[]{:S(2)}, u32[]{:S(2)}) %collective-permute-start.1) | collective-permute-done | bytes 16416 | tf_op jit(solution)/shard_map/cond/branch_0_fun/ppermute | solution.py:507
  42.1 1.1 %collective-permute-done.2.refs_4_ = f32[32,128]{1,0:T(8,128)S(1)} collective-permute-done((f32[32,128]{1,0:T(8,128)S(1)}, f32[32,128]{1,0:T(8,128)S(1)}, u32[]{:S(2)}, u32[]{:S(2)}) %collective-permute-start.2) | collective-permute-done | bytes 16416 | tf_op jit(solution)/shard_map/cond/branch_0_fun/ppermute | solution.py:507
  43.2 0.2 ahead.5
  43.4 1.2 %all-to-all-done.refs_12_ = f32[16,4,128]{2,1,0:T(4,128)S(1)} async-done(((f32[16,4,128]{2,1,0:T(4,128)}), f32[16,4,128]{2,1,0:T(4,128)S(1)}, u32[]{:S(2)}, u32[]{:S(2)}) %all-to-all-start) | async-done | bytes 32800 | tf_op jit(solution)/shard_map/cond/branch_0_fun/all_to_all | solution.py:582
  44.6 2.9 %step.6 = (f32[64,128]{1,0:T(8,128)S(1)}, f32[128,128]{1,0:T(8,128)S(1)}, f32[1,128]{1,0:T(1,128)S(1)}, f32[32,128]{1,0:T(8,128)S(1)}, f32[64,128]{1,0:T(8,128)S(1)}, /*index=5*/f32[16,4,128]{2,1,0:T(4,128)}) custom-call(s16[64,128,128]{2,1,0:T(8,128)(2,1)S(1)} %get-tuple-element.68.refs_0_, f32[64,128]{1,0:T(8,128)S(1)} %get-tuple-element.69.refs_1_, ...), custom_call_target="tpu_custom_call" | custom-call | tf_op jit(solution)/shard_map/cond/branch_0_fun/step/pallas_call | solution.py:453
  47.6 3.7 %all-to-all-start.1 = ((f32[16,4,128]{2,1,0:T(4,128)}), f32[16,4,128]{2,1,0:T(4,128)S(1)}, u32[]{:S(2)}, u32[]{:S(2)}) async-start(f32[16,4,128]{2,1,0:T(4,128)} %get-tuple-element.90), calls=%async_computation.1 | async-start | bytes 65536 | tf_op jit(solution)/shard_map/cond/branch_0_fun/all_to_all | solution.py:582
  51.2 0.4 collective-permute-start.3
  51.7 1.7 %collective-permute-start.4 = (f32[32,128]{1,0:T(8,128)S(1)}, f32[32,128]{1,0:T(8,128)S(1)}, u32[]{:S(2)}, u32[]{:S(2)}) collective-permute-start(f32[32,128]{1,0:T(8,128)S(1)} %get-tuple-element.91.refs_1_), channel_id=1, source_target_pairs={{0,2},{1,3},{2,0},{3,1},{4,6},{5,7},{6,4},{7,5},{8,10},{9,11},{10,... | collective-permute-start | bytes 49160 | tf_op jit(solution)/shard_map/cond/branch_0_fun/ppermute | solution.py:507
  53.3 2.1 %collective-permute-done.4.refs_3_ = f32[32,128]{1,0:T(8,128)S(1)} collective-permute-done((f32[32,128]{1,0:T(8,128)S(1)}, f32[32,128]{1,0:T(8,128)S(1)}, u32[]{:S(2)}, u32[]{:S(2)}) %collective-permute-start.4) | collective-permute-done | bytes 16416 | tf_op jit(solution)/shard_map/cond/branch_0_fun/ppermute | solution.py:507
  55.4 1.1 %collective-permute-done.5.refs_4_ = f32[32,128]{1,0:T(8,128)S(1)} collective-permute-done((f32[32,128]{1,0:T(8,128)S(1)}, f32[32,128]{1,0:T(8,128)S(1)}, u32[]{:S(2)}, u32[]{:S(2)}) %collective-permute-start.5) | collective-permute-done | bytes 16416 | tf_op jit(solution)/shard_map/cond/branch_0_fun/ppermute | solution.py:507
  56.7 1.2 %all-to-all-done.1.refs_12_ = f32[16,4,128]{2,1,0:T(4,128)S(1)} async-done(((f32[16,4,128]{2,1,0:T(4,128)}), f32[16,4,128]{2,1,0:T(4,128)S(1)}, u32[]{:S(2)}, u32[]{:S(2)}) %all-to-all-start.1) | async-done | bytes 32800 | tf_op jit(solution)/shard_map/cond/branch_0_fun/all_to_all | solution.py:582
  57.9 1.8 %step.7 = (f32[16,8,128]{2,1,0:T(8,128)S(1)}, f32[8,128]{1,0:T(8,128)S(1)}) custom-call(s16[64,128,128]{2,1,0:T(8,128)(2,1)S(1)} %get-tuple-element.68.refs_0_, f32[64,128]{1,0:T(8,128)S(1)} %get-tuple-element.69.refs_1_, s32[1,64]{1,0:T(1,128)S(1)} %get-tuple-element.70.refs_2_, f32[1,64]{1,0:T(1,128)S(1)} %get-tuple-element.71.refs_0_.refs_3_, ...), custom_call_target="tpu_custom_call" | custom-call | tf_op jit(solution)/shard_map/cond/branch_0_fun/step/pallas_call | solution.py:453
  59.7 10.4 %all_to_all.26 = f32[16,8,128]{2,1,0:T(8,128)S(1)} all-to-all(f32[16,8,128]{2,1,0:T(8,128)S(1)} %get-tuple-element.97), channel_id=1, replica_groups=mesh['grp'=2,'scen'=4,'blk'=2,'sub'=2] {'scen','blk','sub'}, dimensions={0} | all-to-all | bytes 131072 | tf_op jit(solution)/shard_map/cond/branch_0_fun/all_to_all | solution.py:590
  70.1 0.9 %finish.1 = (f32[256,128]{1,0:T(8,128)}, f32[1,8,128]{2,1,0:T(8,128)}, f32[1,8,128]{2,1,0:T(8,128)}, f32[3]{0:T(128)}) custom-call(f32[16,8,128]{2,1,0:T(8,128)S(1)} %get-tuple-element.201.reply, f32[256,128]{1,0:T(8,128)S(1)} %get-tuple-element.202.base, f32[64,256]{1,0:T(8,128)S(1)} %get-tuple-element.203.place, f32[32,128]{1,0:T(8,128)S(1)} %get-tuple-element.204.y, ...), custom_call_target="tpu_custom_call" | custom-call | tf_op jit(solution)/shard_map/finish/pallas_call | solution.py:453
  (19 shorter events, 0.2 us)
Async XLA Ops:
  0.6 15.1 %copy-start = (f32[256,128]{1,0:T(8,128)S(1)}, f32[256,128]{1,0:T(8,128)}, u32[]{:S(2)}) copy-start(f32[256,128]{1,0:T(8,128)} %cost.3) | copy-start | bytes 393220
  0.6 15.1 %copy-start.1 = (f32[256,128]{1,0:T(8,128)S(1)}, f32[256,128]{1,0:T(8,128)}, u32[]{:S(2)}) copy-start(f32[256,128]{1,0:T(8,128)} %lower.3) | copy-start | bytes 393220
  0.7 15.1 %copy-start.2 = (f32[256,128]{1,0:T(8,128)S(1)}, f32[256,128]{1,0:T(8,128)}, u32[]{:S(2)}) copy-start(f32[256,128]{1,0:T(8,128)} %upper.3) | copy-start | bytes 393220
  0.7 15.1 %copy-start.3 = (f32[256,128]{1,0:T(8,128)S(1)}, f32[256,128]{1,0:T(8,128)}, u32[]{:S(2)}) copy-start(f32[256,128]{1,0:T(8,128)} %first.3) | copy-start | bytes 393220
  2.0 13.8 %all-to-all-start.4 = ((s32[16,1,64]{2,1,0:T(1,128)}), s32[16,1,64]{2,1,0:T(1,128)S(1)}, u32[]{:S(2)}, u32[]{:S(2)}) async-start(s32[16,1,64]{2,1,0:T(1,128)} %broadcast_in_dim.9), calls=%async_computation.4 | async-start | bytes 16384 | tf_op jit(solution)/shard_map/all_to_all | solution.py:471
  10.6 0.7 copy-start.4
  11.3 19.6 %copy-start.7 = (s32[1,64]{1,0:T(1,128)S(1)}, s32[1,64]{1,0:T(1,128)}, u32[]{:S(2)}) copy-start(s32[1,64]{1,0:T(1,128)} %refs_2_.1) | copy-start | bytes 772
  17.2 13.7 %all-to-all-start.5 = ((f32[16,24,128]{2,1,0:T(8,128)}), f32[16,24,128]{2,1,0:T(8,128)S(1)}, u32[]{:S(2)}, u32[]{:S(2)}) async-start(f32[16,24,128]{2,1,0:T(8,128)} %get-tuple-element.181), calls=%async_computation.5 | async-start | bytes 393216 | tf_op jit(solution)/shard_map/all_to_all | solution.py:495
  21.9 5.4 %collective-permute-start.12 = (f32[56,128]{1,0:T(8,128)S(1)}, f32[56,128]{1,0:T(8,128)S(1)}, u32[]{:S(2)}, u32[]{:S(2)}) collective-permute-start(f32[56,128]{1,0:T(8,128)S(1)} %get-tuple-element.182.refs_1_), channel_id=1, source_target_pairs={{0,1},{1,0},{2,3},{3,2},{4,5},{5,4},{6,7},{7,6},{8,9},{9,8},{10,11... | collective-permute-start | bytes 86024 | tf_op jit(solution)/shard_map/ppermute | solution.py:507
  22.4 5.0 %collective-permute-start.13 = (f32[56,128]{1,0:T(8,128)S(1)}, f32[56,128]{1,0:T(8,128)S(1)}, u32[]{:S(2)}, u32[]{:S(2)}) collective-permute-start(f32[56,128]{1,0:T(8,128)S(1)} %get-tuple-element.182.refs_1_), channel_id=1, source_target_pairs={{0,2},{1,3},{2,0},{3,1},{4,6},{5,7},{6,4},{7,5},{8,10},{9,11},{10,... | collective-permute-start | bytes 86024 | tf_op jit(solution)/shard_map/ppermute | solution.py:507
  24.0 3.8 %collective-permute-start.14 = (f32[56,128]{1,0:T(8,128)S(1)}, f32[56,128]{1,0:T(8,128)S(1)}, u32[]{:S(2)}, u32[]{:S(2)}) collective-permute-start(f32[56,128]{1,0:T(8,128)S(1)} %get-tuple-element.182.refs_1_), channel_id=1, source_target_pairs={{0,3},{1,2},{2,1},{3,0},{4,7},{5,6},{6,5},{7,4},{8,11},{9,10},{10,... | collective-permute-start | bytes 86024 | tf_op jit(solution)/shard_map/ppermute | solution.py:507
  34.5 10.1 %all-to-all-start = ((f32[16,4,128]{2,1,0:T(4,128)}), f32[16,4,128]{2,1,0:T(4,128)S(1)}, u32[]{:S(2)}, u32[]{:S(2)}) async-start(f32[16,4,128]{2,1,0:T(4,128)} %get-tuple-element.80), calls=%async_computation | async-start | bytes 65536 | tf_op jit(solution)/shard_map/cond/branch_0_fun/all_to_all | solution.py:582
  38.0 2.0 %collective-permute-start = (f32[32,128]{1,0:T(8,128)S(1)}, f32[32,128]{1,0:T(8,128)S(1)}, u32[]{:S(2)}, u32[]{:S(2)}) collective-permute-start(f32[32,128]{1,0:T(8,128)S(1)} %get-tuple-element.81.refs_1_), channel_id=1, source_target_pairs={{0,1},{1,0},{2,3},{3,2},{4,5},{5,4},{6,7},{7,6},{8,9},{9,8},{10,11... | collective-permute-start | bytes 49160 | tf_op jit(solution)/shard_map/cond/branch_0_fun/ppermute | solution.py:507
  38.3 3.8 %collective-permute-start.1 = (f32[32,128]{1,0:T(8,128)S(1)}, f32[32,128]{1,0:T(8,128)S(1)}, u32[]{:S(2)}, u32[]{:S(2)}) collective-permute-start(f32[32,128]{1,0:T(8,128)S(1)} %get-tuple-element.81.refs_1_), channel_id=1, source_target_pairs={{0,2},{1,3},{2,0},{3,1},{4,6},{5,7},{6,4},{7,5},{8,10},{9,11},{10,... | collective-permute-start | bytes 49160 | tf_op jit(solution)/shard_map/cond/branch_0_fun/ppermute | solution.py:507
  40.0 3.2 %collective-permute-start.2 = (f32[32,128]{1,0:T(8,128)S(1)}, f32[32,128]{1,0:T(8,128)S(1)}, u32[]{:S(2)}, u32[]{:S(2)}) collective-permute-start(f32[32,128]{1,0:T(8,128)S(1)} %get-tuple-element.81.refs_1_), channel_id=1, source_target_pairs={{0,3},{1,2},{2,1},{3,0},{4,7},{5,6},{6,5},{7,4},{8,11},{9,10},{10,... | collective-permute-start | bytes 49160 | tf_op jit(solution)/shard_map/cond/branch_0_fun/ppermute | solution.py:507
  47.6 10.3 %all-to-all-start.1 = ((f32[16,4,128]{2,1,0:T(4,128)}), f32[16,4,128]{2,1,0:T(4,128)S(1)}, u32[]{:S(2)}, u32[]{:S(2)}) async-start(f32[16,4,128]{2,1,0:T(4,128)} %get-tuple-element.90), calls=%async_computation.1 | async-start | bytes 65536 | tf_op jit(solution)/shard_map/cond/branch_0_fun/all_to_all | solution.py:582
  51.2 2.1 %collective-permute-start.3 = (f32[32,128]{1,0:T(8,128)S(1)}, f32[32,128]{1,0:T(8,128)S(1)}, u32[]{:S(2)}, u32[]{:S(2)}) collective-permute-start(f32[32,128]{1,0:T(8,128)S(1)} %get-tuple-element.91.refs_1_), channel_id=1, source_target_pairs={{0,1},{1,0},{2,3},{3,2},{4,5},{5,4},{6,7},{7,6},{8,9},{9,8},{10,11... | collective-permute-start | bytes 49160 | tf_op jit(solution)/shard_map/cond/branch_0_fun/ppermute | solution.py:507
  51.7 3.8 %collective-permute-start.4 = (f32[32,128]{1,0:T(8,128)S(1)}, f32[32,128]{1,0:T(8,128)S(1)}, u32[]{:S(2)}, u32[]{:S(2)}) collective-permute-start(f32[32,128]{1,0:T(8,128)S(1)} %get-tuple-element.91.refs_1_), channel_id=1, source_target_pairs={{0,2},{1,3},{2,0},{3,1},{4,6},{5,7},{6,4},{7,5},{8,10},{9,11},{10,... | collective-permute-start | bytes 49160 | tf_op jit(solution)/shard_map/cond/branch_0_fun/ppermute | solution.py:507
  53.3 3.2 %collective-permute-start.5 = (f32[32,128]{1,0:T(8,128)S(1)}, f32[32,128]{1,0:T(8,128)S(1)}, u32[]{:S(2)}, u32[]{:S(2)}) collective-permute-start(f32[32,128]{1,0:T(8,128)S(1)} %get-tuple-element.91.refs_1_), channel_id=1, source_target_pairs={{0,3},{1,2},{2,1},{3,0},{4,7},{5,6},{6,5},{7,4},{8,11},{9,10},{10,... | collective-permute-start | bytes 49160 | tf_op jit(solution)/shard_map/cond/branch_0_fun/ppermute | solution.py:507
